TPU v7x, 512 devices: a whole 4x8x8 slice. The times are simulated.
512 devices in a mesh: tgt: 64 (over z, y_hi, core), sup: 8 (over x, y_lo).
Axes of the slice: x: 4, y: 8 (y_hi: 4, y_lo: 2; y = y_hi * 2 + y_lo), z: 8, core: 2. Of those that a mesh axis runs over, the one named last changes fastest.
Arguments:
- targets: float32 [512, 3, 1024], P('tgt'), may hold values from -4 to 4
- labels: int32 [512], P('tgt'), may hold values from 0 to 99
- support_slots: float32 [64, 64, 3, 1024], P('tgt', 'sup'), may hold values from -4 to 4
- block_owner: int32 [4], replicated, may hold values from 0 to 63, as said below
- dual_coeffs: float32 [4, 64, 100], P(None, 'sup'), may hold values from -0.15 to 0.15
Outputs:
- predictions: float32 [512, 100], P('tgt')
- support_grad: float32 [4, 64, 3, 1024], P(None, 'sup')
Inputs may be any that keep to these rules, and one draw needn't show every extreme that they name: 4 distinct slot indices, among them 0 and 63; block b is support_slots[block_owner[b]], and the other slots are never read.
All inputs are finite; a program needn't handle non-finite values.
Results may differ from a plain program's by a relative error of at most 0.0001.
Values sent between devices are 32-bit elements; how exact they have to be, the bound alone decides.
No kernel may reach another device: no remote copies, remote signals or barrier semaphores. Data moves between devices by JAX's collectives and lax.ppermute only.
A program may use at most 64 MiB of HBM per device.

v0:
```python
import jax
import jax.numpy as jnp
from jax import lax
from jax.sharding import PartitionSpec as P

SIDE = 32
LAYERS = 3


weight_variance = 1.6
bias_variance = 0.1
loss_weight = 64.0
arcsin_scale = 2.0 / 3.141592653589793


def broadcast(array, axis, root):
    mine = lax.axis_index(axis) == root
    return lax.psum(jnp.where(mine, array, jnp.zeros_like(array)), axis)


def box_sum(states, grid_side):
    length = states.shape[-1]
    column = lax.broadcasted_iota(jnp.int32, (length,), 0) % grid_side
    zero_column = jnp.zeros(states.shape[:-1] + (1,), states.dtype)
    from_left = jnp.where(
        column > 0, jnp.concatenate([zero_column, states[..., :-1]], axis=-1), 0.0
    )
    from_right = jnp.where(
        column < grid_side - 1, jnp.concatenate([states[..., 1:], zero_column], axis=-1), 0.0
    )
    row_sum = states + from_left + from_right
    zero_row = jnp.zeros(states.shape[:-1] + (grid_side,), states.dtype)
    from_above = jnp.concatenate([zero_row, row_sum[..., :-grid_side]], axis=-1)
    from_below = jnp.concatenate([row_sum[..., grid_side:], zero_row], axis=-1)
    return row_sum + from_above + from_below


def self_chain(images):
    squares = images[:, 0, :] * images[:, 0, :]
    for channel in range(1, images.shape[1]):
        squares = squares + images[:, channel, :] * images[:, channel, :]
    variance = weight_variance * box_sum(squares / images.shape[1], SIDE) / 9.0 + bias_variance
    variances = [variance]
    for layer_index in range(1, LAYERS):
        activated = arcsin_scale * jnp.arcsin(2.0 * variance / (1.0 + 2.0 * variance))
        variance = weight_variance * box_sum(activated, SIDE) / 9.0 + bias_variance
        variances.append(variance)
    return variances


def pair_kernel(support, support_variances, targets, target_variances):
    cross_terms = targets[:, 0, :][:, None, :] * support[:, 0, :][None, :, :]
    for channel in range(1, support.shape[1]):
        cross_terms = (
            cross_terms + targets[:, channel, :][:, None, :] * support[:, channel, :][None, :, :]
        )
    preact = weight_variance * box_sum(cross_terms / support.shape[1], SIDE) / 9.0 + bias_variance
    tangent = preact
    activated = preact
    slope = preact
    for layer_index in range(LAYERS):
        product = (1.0 + 2.0 * target_variances[layer_index])[:, None, :] * (
            1.0 + 2.0 * support_variances[layer_index]
        )[None, :, :]
        activated = arcsin_scale * jnp.arcsin(2.0 * preact / jnp.sqrt(product))
        slope = 2.0 * arcsin_scale / jnp.sqrt(product - 4.0 * preact * preact)
        if layer_index + 1 < LAYERS:
            preact_next = weight_variance * box_sum(activated, SIDE) / 9.0 + bias_variance
            tangent = preact_next + weight_variance * box_sum(tangent * slope, SIDE) / 9.0
            preact = preact_next
    return jnp.mean(weight_variance * (activated + tangent * slope) + bias_variance, axis=-1)


def sum_states(images_part, variance_part):
    return lax.psum((images_part, variance_part), "tgt")


def local(targets, labels, support_slots, block_owner, dual_coeffs):
    own_slot = support_slots[0]
    target_variances = self_chain(targets)
    block_count = dual_coeffs.shape[0]
    classes = dual_coeffs.shape[-1]

    def kernel_rows_of(images, variances):
        return pair_kernel(images, variances, targets, target_variances)

    partial_value = jnp.zeros((targets.shape[0], classes), jnp.float32)
    supports = []
    support_sets = []
    self_pullbacks = []
    pullbacks = []
    for block_index in range(block_count):
        support = broadcast(own_slot, "tgt", block_owner[block_index])
        support_variances, self_pullback = jax.vjp(self_chain, support)
        kernel, pullback = jax.vjp(kernel_rows_of, support, support_variances)
        pullbacks.append(pullback)
        supports.append(support)
        support_sets.append(support_variances)
        self_pullbacks.append(self_pullback)
        partial_value = partial_value + jnp.dot(
            kernel, dual_coeffs[block_index], precision=lax.Precision.HIGHEST
        )
    predictions = lax.psum(partial_value, "sup")
    onehot = (labels[:, None] == lax.broadcasted_iota(jnp.int32, (1, classes), 1)).astype(
        jnp.float32
    )
    residual_error = loss_weight * (predictions - onehot)
    image_terms = []
    variance_terms = []
    for block_index in range(block_count):
        pair_weights = jnp.dot(
            residual_error, dual_coeffs[block_index].T, precision=lax.Precision.HIGHEST
        )
        grad_images, grad_variances = pullbacks[block_index](pair_weights)
        image_terms.append(grad_images)
        variance_terms.append(jnp.stack(grad_variances))
    gradients = []
    for block_index in range(block_count):
        summed_images, summed_variances = sum_states(
            image_terms[block_index], variance_terms[block_index]
        )
        variance_list = [summed_variances[layer_index] for layer_index in range(LAYERS)]
        gradients.append(summed_images + self_pullbacks[block_index](variance_list)[0])
    return (predictions, jnp.stack(gradients))


def solution(mesh):
    return jax.shard_map(
        local,
        mesh=mesh,
        in_specs=(
            P("tgt", None, None),
            P("tgt"),
            P("tgt", "sup", None, None),
            P(),
            P(None, "sup", None),
        ),
        out_specs=(P("tgt", None), P(None, "sup", None, None)),
        check_vma=False,
    )
```

profile of v0, /device:TPU:1, one launch (start us, length us, event | category | flops | bytes accessed | tf_op | source)
XLA Modules:
  0.0 1204.3 jit_solution(16650220429389493855)
XLA Ops:
  7.9 0.7 fusion.412
  11.2 1.6 select_bitcast_fusion.3
  13.0 0.7 copy-done.33
  14.4 545.0 %all-reduce.299.cloned.1.call-done = (f32[8,3,1024]{2,0,1:T(8,128)}, f32[8,3,1024]{2,0,1:T(8,128)}, f32[8,3,1024]{2,0,1:T(8,128)}, f32[8,3,1024]{2,0,1:T(8,128)}) async-done(((f32[8,3,1024]{2,0,1:T(8,128)}, f32[8,3,1024]{2,0,1:T(8,128)}, f32[8,3,1024]{2,0,1:T(8,128)}, f32[8,3,1024]{2,0,1:T(8,128)}), (f32[8,3,1024]{2,0,1:T(8,128)}, f32[8,3,1024]{2,0,1:T(8,128)}, f32[8,3,1024]{2,0,1:T(8,128)}, ...) | async-done | bytes 393232 | tf_op jit(solution)/shard_map/psum | solution.py:18
  559.4 0.9 add_multiply_fusion.34
  560.4 0.9 copy-done.7
  571.4 1.4 fusion.227
  573.2 1.2 add_multiply_fusion.15
  578.1 2.1 add_multiply_fusion.1
  581.3 1.2 add_multiply_fusion.13
  584.9 4.2 add_reduce_fusion
  589.7 15.0 %psum.95 = f32[8,100]{1,0:T(8,128)S(1)} all-reduce(f32[8,100]{1,0:T(8,128)S(1)} %convolution_add_fusion), channel_id=1, replica_groups=mesh['tgt'=64,'sup'=8] {'sup'}, use_global_device_ids=true, to_apply=%region_8.9 | all-reduce | flops 800 | bytes 6400 | tf_op jit(solution)/shard_map/psum | solution.py:103
  604.8 0.9 broadcast_multiply_fusion.13
  605.7 0.9 broadcast_multiply_fusion.12
  606.6 0.9 broadcast_multiply_fusion.11
  607.6 0.9 broadcast_multiply_fusion.14
  608.5 2.8 fusion.206
  612.2 0.8 copy-done.1
  615.0 0.9 slice_select_fusion.15
  615.9 0.9 fusion.205
  616.8 0.9 fusion.211
  617.7 0.9 fusion.155
  620.5 1.0 fusion.204
  621.5 1.0 fusion.146
  622.5 0.9 fusion.125
  626.0 0.9 fusion.207
  626.9 1.0 fusion.116
  634.6 542.6 %all-reduce.297.cloned.1.call-done = (f32[8,3,1024]{2,0,1:T(8,128)}, f32[3,8,1024]{2,1,0:T(8,128)}, f32[8,3,1024]{2,0,1:T(8,128)}, f32[3,8,1024]{2,1,0:T(8,128)}...) async-done(((f32[8,3,1024]{2,0,1:T(8,128)}, f32[3,8,1024]{2,1,0:T(8,128)}, f32[8,3,1024]{2,0,1:T(8,128)}, ...) | async-done | bytes 786448 | tf_op jit(solution)/shard_map/psum | solution.py:75
  1177.3 0.8 fusion.240
  1178.1 0.8 fusion.247
  1179.4 0.7 copy-done.40
  1180.3 0.7 copy-done.46
  1181.1 0.8 copy-done.50
  1183.3 0.7 copy-done.28
  1184.1 0.7 copy-done.32
  1185.0 0.7 copy-done.30
  1185.8 0.8 copy-done.47
  1187.1 0.8 copy-done.10
  1188.0 0.9 copy-done.8
  1188.9 0.9 copy-done.6
  1189.9 0.7 copy-done.42
  1191.0 0.7 copy-done.26
  1192.0 0.8 copy-done.4
  1192.9 0.9 copy-done.57
  1193.8 0.9 copy-done.56
  1194.7 0.9 copy-done.55
  1195.6 0.9 copy-done.54
  1196.5 0.8 pad_maximum_fusion
  (339 shorter events, 37.3 us)
Async XLA Ops:
  7.2 552.2 %all-reduce.299.cloned.1.call-start = ((), (), s32[]{:S(2)}) async-start(), calls=%async_computation.1 | async-start | bytes 786432 | tf_op jit(solution)/shard_map/psum | solution.py:18
  12.8 0.9 copy-start.33
  12.8 1164.4 %all-reduce.297.cloned.1.call-start = ((), (), s32[]{:S(2)}) async-start(), calls=%async_computation | async-start | bytes 1572864 | tf_op jit(solution)/shard_map/psum | solution.py:75
  559.4 1.0 copy-start.3
  559.4 1.0 copy-start.5
  560.4 0.9 copy-start.7
  560.4 0.9 copy-start.9
  562.0 11.2 copy-start.17
  563.7 17.7 %copy-start.21 = (f32[8,1024]{1,0:T(8,128)}, f32[8,1024]{1,0:T(8,128)S(1)}, u32[]{:S(2)}) copy-start(f32[8,1024]{1,0:T(8,128)S(1)} %get-tuple-element.409) | copy-start | bytes 98308
  564.3 9.0 copy-start.15
  565.2 0.8 copy-start.39
  566.7 14.6 %copy-start.19 = (f32[8,1024]{1,0:T(8,128)}, f32[8,1024]{1,0:T(8,128)S(1)}, u32[]{:S(2)}) copy-start(f32[8,1024]{1,0:T(8,128)S(1)} %get-tuple-element.407) | copy-start | bytes 98308
  567.8 10.3 copy-start.13
  568.9 9.2 copy-start.11
  584.4 4.7 copy-start.37
  584.9 4.2 copy-start.58
  604.8 2.8 copy-start.60
  604.8 3.7 copy-start
  612.0 1.0 copy-start.1
  612.0 1.0 copy-start.2
  612.0 1.0 copy-start.24
  612.0 1.0 copy-start.38
  614.9 0.9 copy-start.20
  615.0 0.9 copy-start.22
  615.9 0.9 copy-start.12
  615.9 0.9 copy-start.14
  619.8 0.8 copy-start.18
  625.2 0.8 copy-start.16
  630.8 0.8 copy-start.52
  630.8 0.8 copy-start.53
  1177.3 1.6 copy-start.48
  1177.3 1.6 copy-start.49
  1179.3 0.8 copy-start.40
  1180.2 0.8 copy-start.46
  1181.0 0.9 copy-start.50
  1182.2 0.8 copy-start.44
  1183.2 0.8 copy-start.28
  1184.0 0.8 copy-start.32
  1185.7 0.9 copy-start.47
  1187.0 0.9 copy-start.10
  1187.9 0.9 copy-start.8
  1188.9 0.9 copy-start.6
  1190.9 0.8 copy-start.26
  1191.9 0.9 copy-start.4
  1192.9 0.9 copy-start.57
  1193.8 0.9 copy-start.56
  1194.7 0.9 copy-start.55
  1195.6 0.9 copy-start.54
  (15 other events, 9.6 us)
Sparse Core Ops, SparseCore 0:
  12.9 546.3 all-reduce.298
  634.8 542.4 all-reduce.296
where the time goes:
time: 1210 us; the launch traced here: 1200 us
  waiting for transfers between devices  1090 us (90%)
  other arithmetic  46 us (4%)
  local copies, waits for them, and re-layouts  33.1 us (3%)
  between operations  18.3 us (2%)
  blocking collectives  15 us (1%)
    psum x1, waiting for transfers between devices, broadcast(): return lax.psum(jnp.where(mine, array, jnp.zeros_like(array)), axis)  545 us
    psum x1, waiting for transfers between devices, sum_states(): return lax.psum((images_part, variance_part), 'tgt')  543 us
  transfers between devices with their start and end apart: 2, of which 2 were waited for; matrix products, arithmetic and copies ran while one was open for 0% of the time, Pallas kernels for 0%

commit v1 on v0

v1 whole, which is shorter than its diff:
```python
import functools

import jax
import jax.numpy as jnp
from jax import lax
from jax.experimental import pallas as pl
from jax.experimental.pallas import tpu as pltpu
from jax.sharding import PartitionSpec as P

LANES = 128
ROWS = 8
PIX = 1024
CH = 3
ALPHA = 1.6 / 9.0
W = 1.6
BIAS = 0.1
LOSS = 64.0
Q = 2.0 / 3.141592653589793

WIDE = (1.000000016156341, 0.16666297522317508, 0.07513696096432515, 0.04275936583215643,
        0.04244150116676571, -0.015453175442799802, 0.0693722411926219)
NARROW = (1.000000019010712, 0.16666188274704566, 0.07519150147740127, 0.04200062838628592,
          0.04465464851544397)


def half_arcsin(z, o, r, coefficients):
    y = z * lax.rsqrt(0.5 + 0.5 * (o * r))
    y2 = y * y
    scaled = [Q * c * 0.25**k for k, c in enumerate(coefficients)]
    total = scaled[-1]
    for c in scaled[-2::-1]:
        total = total * y2 + c
    return y * total


def lane_masks():
    lane = lax.broadcasted_iota(jnp.int32, (8, LANES), 1)
    x = lane % 32
    return (x > 0, x < 31, lane >= 32, lane < 96, [lane // 32 == k for k in range(1, 4)])


def box(v, masks):
    left, right, above, below, _ = masks
    r = []
    for a in v:
        r.append(
            a
            + jnp.where(left, pltpu.roll(a, 1, 1), 0.0)
            + jnp.where(right, pltpu.roll(a, LANES - 1, 1), 0.0)
        )
    first = jnp.where(above, pltpu.roll(r[7], 32, 1), 0.0)
    last = jnp.where(below, pltpu.roll(r[0], LANES - 32, 1), 0.0)
    r = [first] + r + [last]
    out = []
    for k in range(0, 8, 2):
        pair = r[k + 1] + r[k + 2]
        out.append(r[k] + pair)
        out.append(pair + r[k + 3])
    return out


def interleave(nat, masks):
    groups = masks[4]
    out = []
    for r in range(8):
        m, q = r // 4, r % 4
        v = None
        for y in range(4):
            a = nat[2 * y + m]
            shift = (32 * (y - q)) % LANES
            a = a if shift == 0 else pltpu.roll(a, shift, 1)
            v = a if v is None else jnp.where(groups[y - 1], a, v)
        out.append(v)
    return out


def deinterleave(v, masks):
    groups = masks[4]
    out = []
    for m in range(8):
        y, h = m // 2, m % 2
        o = None
        for q in range(4):
            a = v[4 * h + q]
            shift = (32 * (q - y)) % LANES
            a = a if shift == 0 else pltpu.roll(a, shift, 1)
            o = a if o is None else jnp.where(groups[q - 1], a, o)
        out.append(o)
    return out


def chain(channels, masks):
    squares = [a * a + b * b + d * d for a, b, d in zip(*channels)]
    n = [(ALPHA / CH) * a + BIAS for a in box(squares, masks)]
    factors, slopes = [], []
    for h in range(3):
        b = [lax.rsqrt(1.0 + 2.0 * a) for a in n]
        factors.append(b)
        if h < 2:
            act = []
            slope = []
            for a, bb in zip(n, b):
                inv = bb * bb
                z = 2.0 * a * inv
                rr = lax.rsqrt(1.0 + 4.0 * a)
                o = (1.0 + 4.0 * a) * (inv * inv)
                r = (1.0 + 2.0 * a) * rr
                act.append(half_arcsin(z, o, r, WIDE if h == 0 else NARROW))
                slope.append(2.0 * Q * inv * rr)
            slopes.append(slope)
            n = [ALPHA * a + BIAS for a in box(act, masks)]
    return factors, slopes


def main_kernel(core_ref, own_ref, other_ref, rows_ref, coef_ref, label_ref,
                parts_ref, unit_ref, tgt_ref, sup_ref, kt_ref):
    masks = lane_masks()
    core = core_ref[0]
    step = pl.program_id(0)

    @pl.when(step == 0)
    def _():
        for half, ref in enumerate((own_ref, other_ref)):
            chans = []
            for ch in range(CH):
                nat = [ref[:, ch, m * LANES:(m + 1) * LANES] for m in range(8)]
                chans.append(interleave(nat, masks))
            factors, _ = chain(chans, masks)
            for ch in range(CH):
                for r in range(8):
                    tgt_ref[half, ch, r] = chans[ch][r]
            for h in range(3):
                for r in range(8):
                    tgt_ref[half, 3 + h, r] = 2.0 * factors[h][r]
        for g in range(2):
            chans = []
            for ch in range(CH):
                nat = []
                for m in range(8):
                    pieces = [
                        rows_ref[pl.ds(m * 48 + (2 * g + b) * 3 + ch, 4, stride=12), :]
                        for b in range(2)
                    ]
                    nat.append(jnp.concatenate(pieces, axis=0))
                chans.append(interleave(nat, masks))
            factors, slopes = chain(chans, masks)
            for ch in range(CH):
                for r in range(8):
                    sup_ref[g, ch, r] = chans[ch][r]
            for h in range(3):
                for r in range(8):
                    sup_ref[g, 3 + h, r] = factors[h][r]
            for h in range(2):
                for r in range(8):
                    sup_ref[g, 6 + h, r] = slopes[h][r]
        kt_ref[...] = jnp.zeros_like(kt_ref)

    g = step // 2
    half = step % 2
    lane = lax.broadcasted_iota(jnp.int32, (8, LANES), 1)
    R = range(8)

    def pair(t, carry):
        def tgt(k, r):
            return jnp.broadcast_to(tgt_ref[half, k, r, pl.ds(t, 1), :], (8, LANES))

        def layer(h, S, theta):
            p2 = [tgt(3 + h, r) * sup_ref[g, 3 + h, r] for r in R]
            z = [p * s for p, s in zip(p2, S)]
            o = [1.0 - a * a for a in z]
            rt = [lax.rsqrt(a) for a in o]
            act = [half_arcsin(a, b, c, WIDE if h == 0 else NARROW) for a, b, c in zip(z, o, rt)]
            u = [Q * a for a in rt]
            D = [a * b for a, b in zip(p2, u)]
            f = [a * b * (c * c) for a, b, c in zip(p2, theta, rt)]
            return z, act, u, D, f

        cross = []
        for r in R:
            cross.append(tgt(0, r) * sup_ref[g, 0, r] + tgt(1, r) * sup_ref[g, 1, r]
                         + tgt(2, r) * sup_ref[g, 2, r])
        S1 = [(ALPHA / CH) * a + BIAS for a in box(cross, masks)]
        z1, A1, u1, D1, f1 = layer(0, S1, S1)
        S2 = [ALPHA * a + BIAS for a in box(A1, masks)]
        T2 = [s + ALPHA * a for s, a in zip(S2, box([x * y for x, y in zip(S1, D1)], masks))]
        z2, A2, u2, D2, f2 = layer(1, S2, T2)
        S3 = [ALPHA * a + BIAS for a in box(A2, masks)]
        T3 = [s + ALPHA * a for s, a in zip(S3, box([x * y for x, y in zip(T2, D2)], masks))]
        z3, A3, u3, D3, f3 = layer(2, S3, T3)
        total = None
        for r in R:
            term = A3[r] + T3[r] * D3[r]
            total = term if total is None else total + term
        ksum = jnp.sum(total, axis=1, keepdims=True) * (W / PIX) + BIAS
        column = half * 8 + t
        kt_ref[g] = jnp.where(lane == column, ksum, kt_ref[g])

        gt = D3
        gs = []
        for r in R:
            unit_ref[0, t, 3, r] = u3[r] * (z3[r] + f3[r])
            gs.append(D3[r] * (2.0 + z3[r] * f3[r]))
        ga = [ALPHA * a for a in box(gs, masks)]
        gp = [ALPHA * a for a in box(gt, masks)]
        gt = []
        gs = []
        for r in R:
            e = gp[r] * f2[r]
            unit_ref[0, t, 2, r] = u2[r] * (z2[r] * ga[r] + e)
            gt.append(gp[r] * D2[r])
            gs.append(D2[r] * (ga[r] + gp[r] + z2[r] * e))
        ga = [ALPHA * a for a in box(gs, masks)]
        gp = [ALPHA * a for a in box(gt, masks)]
        gs = []
        for r in R:
            e = gp[r] * f1[r]
            unit_ref[0, t, 1, r] = u1[r] * (z1[r] * ga[r] + e)
            gs.append(D1[r] * (ga[r] + gp[r] + z1[r] * e))
        gx = box(gs, masks)
        for r in R:
            unit_ref[0, t, 0, r] = gx[r]
        return carry

    lax.fori_loop(0, 8, pair, 0)

    @pl.when(step == 3)
    def _():
        part = None
        for g2 in range(2):
            rows = jnp.concatenate(
                [coef_ref[2 * g2 + b, pl.ds(core * 4, 4), :] for b in range(2)], axis=0
            )
            rows = jnp.concatenate([rows, jnp.zeros((8, LANES - rows.shape[1]), jnp.float32)], axis=1)
            term = lax.dot_general(
                kt_ref[g2], rows, (((0,), (0,)), ((), ())),
                precision=lax.Precision.HIGHEST, preferred_element_type=jnp.float32,
            )
            part = term if part is None else part + term
        own, other = part[0:8], part[8:16]
        own = jnp.where(lane == LANES - 1, label_ref[...], own)
        for peer in range(16):
            parts_ref[peer, pl.ds(pl.multiple_of(core * 8, 8), 8), :] = own
            parts_ref[peer, pl.ds(pl.multiple_of((1 - core) * 8, 8), 8), :] = other


def weigh_kernel(core_ref, parts_ref, unit_ref, tgt_ref, sup_ref, coef_ref,
                 pred_ref, grad_ref, weight_ref, acc_ref):
    masks = lane_masks()
    core = core_ref[0]
    step = pl.program_id(0)
    lane = lax.broadcasted_iota(jnp.int32, (8, LANES), 1)
    classes = coef_ref.shape[2]

    @pl.when(step == 0)
    def _():
        def total(start):
            start = pl.multiple_of(start, 8)
            v = parts_ref[0, pl.ds(start, 8), :]
            for peer in range(1, 16):
                v = v + parts_ref[peer, pl.ds(start, 8), :]
            return v

        errs = []
        for k, start in enumerate((core * 8, (1 - core) * 8)):
            v = total(start)
            label = v[:, LANES - 1:LANES]
            onehot = jnp.where(lane.astype(jnp.float32) == label, 1.0, 0.0)
            if k == 0:
                pred_ref[...] = v
            errs.append(jnp.where(lane < classes, LOSS * (v - onehot), 0.0))
        err = jnp.concatenate(errs, axis=0)
        for g in range(2):
            rows = jnp.concatenate(
                [coef_ref[2 * g + b, pl.ds(core * 4, 4), :] for b in range(2)], axis=0
            )
            rows = jnp.concatenate([rows, jnp.zeros((8, LANES - classes), jnp.float32)], axis=1)
            wt = lax.dot_general(
                rows, err, (((1,), (1,)), ((), ())),
                precision=lax.Precision.HIGHEST, preferred_element_type=jnp.float32,
            )
            for t in range(16):
                weight_ref[g, t] = jnp.broadcast_to(wt[:, t:t + 1] * (W / PIX), (8, LANES))

    g = step // 2
    half = step % 2

    def row(r, carry):
        acc = [None] * 6
        for t in range(8):
            w = weight_ref[g, half * 8 + t]
            x = w * unit_ref[0, t, 0, r]
            terms = [
                x * jnp.broadcast_to(tgt_ref[half, ch, r, t:t + 1, :], (8, LANES))
                for ch in range(CH)
            ] + [w * unit_ref[0, t, 1 + h, r] for h in range(3)]
            acc = [b if a is None else a + b for a, b in zip(acc, terms)]
        for k in range(6):
            acc_ref[half, k, r] = acc[k]
        return carry

    lax.fori_loop(0, 8, row, 0)

    @pl.when(half == 1)
    def _():
        R = range(8)

        def variance(h):
            return [
                -(sup_ref[g, 3 + h, r] * sup_ref[g, 3 + h, r])
                * (acc_ref[0, 3 + h, r] + acc_ref[1, 3 + h, r])
                for r in R
            ]

        gn = variance(2)
        for h in (1, 0):
            back = box(gn, masks)
            own = variance(h)
            gn = [own[r] + ALPHA * back[r] * sup_ref[g, 6 + h, r] for r in R]
        back = box(gn, masks)
        for ch in range(CH):
            v = [
                (ALPHA / CH) * (acc_ref[0, ch, r] + acc_ref[1, ch, r] + 2.0 * sup_ref[g, ch, r] * back[r])
                for r in R
            ]
            nat = deinterleave(v, masks)
            for m in range(8):
                for b in range(2):
                    grad_ref[pl.ds(m * 48 + (2 * g + b) * 3 + ch, 4, stride=12), :] = nat[m][4 * b:4 * b + 4]


VMEM = pltpu.MemorySpace.VMEM
SMEM = pltpu.MemorySpace.SMEM


def whole(shape):
    return pl.BlockSpec(shape, lambda i: (0,) * len(shape))


def main_call(core, own, other, rows, coef, label):
    f32 = jnp.float32
    return pl.pallas_call(
        main_kernel,
        grid=(4,),
        in_specs=[
            pl.BlockSpec(memory_space=SMEM),
            whole((8, CH, PIX)), whole((8, CH, PIX)), whole((384, LANES)),
            whole(coef.shape), whole((8, 1)),
        ],
        out_specs=[
            whole((16, 16, LANES)),
            pl.BlockSpec((1, 8, 4, 8, 8, LANES), lambda i: (i, 0, 0, 0, 0, 0)),
            whole((2, 6, 8, 8, LANES)),
            whole((2, 8, 8, 8, LANES)),
        ],
        out_shape=[
            jax.ShapeDtypeStruct((16, 16, LANES), f32),
            jax.ShapeDtypeStruct((4, 8, 4, 8, 8, LANES), f32),
            jax.ShapeDtypeStruct((2, 6, 8, 8, LANES), f32),
            jax.ShapeDtypeStruct((2, 8, 8, 8, LANES), f32),
        ],
        scratch_shapes=[pltpu.VMEM((2, 8, LANES), f32)],
        name="pairs",
    )(core, own, other, rows, coef, label)


def weigh_call(core, parts, unit, tgt, sup, coef):
    f32 = jnp.float32
    return pl.pallas_call(
        weigh_kernel,
        grid=(4,),
        in_specs=[
            pl.BlockSpec(memory_space=SMEM),
            whole((16, 16, LANES)),
            pl.BlockSpec((1, 8, 4, 8, 8, LANES), lambda i: (i, 0, 0, 0, 0, 0)),
            whole((2, 6, 8, 8, LANES)),
            whole((2, 8, 8, 8, LANES)),
            whole(coef.shape),
        ],
        out_specs=[whole((8, LANES)), whole((384, LANES))],
        out_shape=[
            jax.ShapeDtypeStruct((8, LANES), f32),
            jax.ShapeDtypeStruct((384, LANES), f32),
        ],
        scratch_shapes=[pltpu.VMEM((2, 16, 8, LANES), f32), pltpu.VMEM((2, 6, 8, 8, LANES), f32)],
        name="weigh",
    )(core, parts, unit, tgt, sup, coef)


def local(tgt_n, sup_n, targets, labels, support_slots, block_owner, dual_coeffs):
    blocks = dual_coeffs.shape[0]
    classes = dual_coeffs.shape[2]
    index = lax.axis_index("tgt")
    core = (index % 2)[None].astype(jnp.int32)
    partner = [(t, t ^ 1) for t in range(tgt_n)]
    planes = [[t for t in range(tgt_n) if t % 2 == c] for c in range(2)]
    sets = [
        [t * sup_n + s for t in (2 * k, 2 * k + 1) for s in range(sup_n)] for k in range(tgt_n // 2)
    ]
    other = lax.ppermute(targets, "tgt", partner)
    slot = support_slots[0].reshape(2, 4, CH, 8, LANES)
    slot = slot.transpose(3, 1, 0, 2, 4).reshape(tgt_n, CH, LANES)
    got = lax.all_to_all(slot, "tgt", 0, 0, tiled=True)
    mine = jnp.concatenate(
        [lax.dynamic_slice_in_dim(got, block_owner[b], 1, 0) for b in range(blocks)], axis=0
    ).reshape(1, blocks * CH, LANES)
    half_n = tgt_n // 2
    rows = lax.all_to_all(
        jnp.broadcast_to(mine, (half_n, blocks * CH, LANES)), "tgt", 0, 0,
        axis_index_groups=planes, tiled=True,
    ).reshape(half_n * blocks * CH, LANES)
    first = lax.axis_index("sup") == 0
    label = jnp.where(first, labels.astype(jnp.float32), 0.0)[:, None]
    parts, unit, tgt, sup = main_call(core, targets, other, rows, dual_coeffs, label)
    parts = lax.all_to_all(
        parts, ("tgt", "sup"), 0, 0, axis_index_groups=sets, tiled=True
    )
    pred, grad = weigh_call(core, parts, unit, tgt, sup, dual_coeffs)
    grad = lax.all_to_all(
        grad.reshape(half_n, blocks * CH, LANES), "tgt", 0, 0, axis_index_groups=planes, tiled=True
    )
    piece = jnp.sum(grad, axis=0, keepdims=True)
    full = lax.all_to_all(
        jnp.broadcast_to(piece, (half_n, blocks * CH, LANES)), "tgt", 0, 0,
        axis_index_groups=planes, tiled=True,
    )
    theirs = lax.ppermute(full, "tgt", partner)
    even = jnp.where(core[0] == 0, full, theirs)
    odd = jnp.where(core[0] == 0, theirs, full)
    both = jnp.stack([even, odd]).reshape(2, 8, 4, blocks, CH, LANES)
    out = both.transpose(3, 0, 2, 4, 1, 5).reshape(blocks, 8, CH, PIX)
    return pred[:, :classes], out


def solution(mesh):
    return jax.shard_map(
        functools.partial(local, mesh.shape["tgt"], mesh.shape["sup"]),
        mesh=mesh,
        in_specs=(
            P("tgt", None, None),
            P("tgt"),
            P("tgt", "sup", None, None),
            P(),
            P(None, "sup", None),
        ),
        out_specs=(P("tgt", None), P(None, "sup", None, None)),
        check_vma=False,
    )
```

time: 1210 us -> 153 us (0.13)
  waiting for transfers between devices: 1090 us -> 12.5 us
  other arithmetic: 46 us -> 0.88 us
  Pallas kernels: 0 us -> 40.9 us
  starting transfers between devices: 0.08 us -> 33.1 us
  blocking collectives: 15 us -> 47.4 us
  local copies, waits for them, and re-layouts: 33.1 us -> 8.8 us
    psum x2 -> x0, waiting for transfers between devices: 1090 us -> none  [the longest x1 545 us: broadcast(): return lax.psum(jnp.where(mine, array, jnp.zeros_like(array)), axis)]
    all_to_all x0 -> x3, blocking collectives: none -> 47.4 us  [the longest x1 18.4 us: local(): lax.all_to_all(jnp.broadcast_to(piece, (half_n, blocks * CH, LANES)), 'tg...]
    pallas_call x0 -> x2, Pallas kernels: none -> 40.9 us  [the longest x1 35 us: main_call(): pl.pallas_call(main_kernel, grid=(4,), in_specs=[pl.BlockSpec(memory_spac...]
    all_to_all x0 -> x2, starting transfers between devices: none -> 25.5 us  [the longest x1 17.6 us: local(): got = lax.all_to_all(slot, 'tgt', 0, 0, tiled=True)]
    unnamed x122 -> x6, local copies, waits for them, and re-layouts: 21 us -> 2.53 us
    psum x1 -> x0, blocking collectives: 15 us -> none  [local(): predictions = lax.psum(partial_value, 'sup')]
    mul x43 -> x0, other arithmetic: 14.8 us -> none  [the longest x3 4.54 us: pair_kernel(): activated = arcsin_scale * jnp.arcsin(2.0 * preact / jnp.sqrt(product))]
  transfers between devices with their start and end apart: 2 -> 4, of which waited for: 2 -> 3; matrix products, arithmetic and copies ran while one was open for 0% -> 3% of each run, Pallas kernels for 0% -> 0%
where the time goes in v1:
time: 153 us; the launch traced here: 152 us
  blocking collectives  47.4 us (31%)
  Pallas kernels  40.9 us (27%)
  starting transfers between devices  33.1 us (22%)
  waiting for transfers between devices  12.5 us (8%)
  local copies, waits for them, and re-layouts  8.8 us (6%)
  between operations  8.34 us (5%)
    pallas_call x1, Pallas kernels, main_call(): pl.pallas_call(main_kernel, grid=(4,), in_specs=[pl.BlockSpec(memory_spac...  35 us
    all_to_all x1, blocking collectives, local(): lax.all_to_all(jnp.broadcast_to(piece, (half_n, blocks * CH, LANES)), 'tg...  18.4 us
    all_to_all x1, starting transfers between devices, local(): got = lax.all_to_all(slot, 'tgt', 0, 0, tiled=True)  17.6 us
    all_to_all x1, blocking collectives, local(): lax.all_to_all(grad.reshape(half_n, blocks * CH, LANES), 'tgt', 0, 0, axi...  16.1 us
    all_to_all x1, blocking collectives, local(): lax.all_to_all(parts, ('tgt', 'sup'), 0, 0, axis_index_groups=sets, tiled...  12.9 us
    all_to_all x1, starting transfers between devices, local(): lax.all_to_all(jnp.broadcast_to(mine, (half_n, blocks * CH, LANES)), 'tgt...  7.85 us
    all_to_all x1, waiting for transfers between devices, local(): lax.all_to_all(jnp.broadcast_to(mine, (half_n, blocks * CH, LANES)), 'tgt...  7.44 us
    pallas_call x1, Pallas kernels, weigh_call(): pl.pallas_call(weigh_kernel, grid=(4,), in_specs=[pl.BlockSpec(memory_spa...  5.89 us
  transfers between devices with their start and end apart: 4, of which 3 were waited for; matrix products, arithmetic and copies ran while one was open for 3% of the time, Pallas kernels for 0%

profile of v1, /device:TPU:1, one launch (start us, length us, event | category | flops | bytes accessed | tf_op | source)
XLA Modules:
  0.0 151.9 jit_solution(15676345660769764545)
XLA Ops:
  0.6 0.9 copy.30
  1.5 0.1 copy.22
  1.6 0.7 copy.23
  2.4 17.6 %all-to-all-start = ((f32[64,3,128]{2,1,0:T(4,128)}), f32[64,3,128]{2,1,0:T(4,128)S(1)}, u32[]{:S(2)}, u32[]{:S(2)}) async-start(f32[64,3,128]{2,1,0:T(4,128)} %copy.23), calls=%async_computation | async-start | bytes 262144 | tf_op jit(solution)/shard_map/all_to_all | solution.py:402
  20.0 1.5 fusion.1
  29.1 4.0 %all-to-all-done = f32[64,3,128]{2,1,0:T(4,128)S(1)} async-done(((f32[64,3,128]{2,1,0:T(4,128)}), f32[64,3,128]{2,1,0:T(4,128)S(1)}, u32[]{:S(2)}, u32[]{:S(2)}) %all-to-all-start) | async-done | bytes 98336 | tf_op jit(solution)/shard_map/all_to_all | solution.py:402
  33.1 0.7 broadcast_in_dim.25
  33.9 7.8 %all-to-all-start.1 = ((f32[32,12,128]{2,1,0:T(8,128)}), f32[32,12,128]{2,1,0:T(8,128)S(1)}, u32[]{:S(2)}, u32[]{:S(2)}) async-start(f32[32,12,128]{2,1,0:T(8,128)} %broadcast_in_dim.25), calls=%async_computation.1 | async-start | bytes 524288 | tf_op jit(solution)/shard_map/all_to_all | solution.py:407
  41.7 1.0 copy.24.own_ref
  42.7 0.0 copy-start
  42.7 2.6 %collective-permute-start = (f32[8,3,1024]{2,1,0:T(4,128)S(1)}, f32[8,3,1024]{2,1,0:T(4,128)S(1)}, u32[]{:S(2)}, u32[]{:S(2)}) collective-permute-start(f32[8,3,1024]{2,1,0:T(4,128)S(1)} %copy.24.own_ref), channel_id=1, source_target_pairs={{0,8},{8,0},{16,24},{24,16},{32,40},{40,32},{48,56},{56,48},{64,72... | collective-permute-start | bytes 294920 | tf_op jit(solution)/shard_map/ppermute | solution.py:399
  45.3 0.7 fusion
  45.9 0.7 copy.25.label_ref
  46.6 7.4 %all-to-all-done.1 = f32[32,12,128]{2,1,0:T(8,128)S(1)} async-done(((f32[32,12,128]{2,1,0:T(8,128)}), f32[32,12,128]{2,1,0:T(8,128)S(1)}, u32[]{:S(2)}, u32[]{:S(2)}) %all-to-all-start.1) | async-done | bytes 196640 | tf_op jit(solution)/shard_map/all_to_all | solution.py:407
  54.1 0.7 reshape.25.rows_ref
  54.8 0.0 collective-permute-done.other_ref
  54.8 0.0 copy-start.1
  54.8 0.0 copy-done
  54.8 0.7 copy-done.1
  55.4 35.0 %pairs.1 = (f32[16,16,128]{2,1,0:T(8,128)}, f32[4,8,4,8,8,128]{5,4,3,2,1,0:T(8,128)}, f32[2,6,8,8,128]{4,3,2,1,0:T(8,128)}, f32[2,8,8,8,128]{4,3,2,1,0:T(8,128)}) custom-call(s32[1]{0:T(128)} %bitcast.core_ref, f32[8,3,1024]{2,1,0:T(4,128)} %copy-done, f32[8,3,1024]{2,1,0:T(4,128)} %copy-done.1, f32[384,128]{1,0:T(8,128)} %reshape.25.rows_ref, ...), custom_call_target="tpu_custom_call" | custom-call | tf_op jit(solution)/shard_map/pairs/pallas_call | solution.py:341
  90.4 12.9 %all_to_all.25.parts_ref = f32[16,16,128]{2,1,0:T(8,128)} all-to-all(f32[16,16,128]{2,1,0:T(8,128)} %get-tuple-element.8), channel_id=1, replica_groups={{0,1,2,3,4,5,6,7,8,9,10,11,12,13,14,15},{16,17,18,19,20,21,22,23,24,25,..., dimensions={0} | all-to-all | bytes 262144 | tf_op jit(solution)/shard_map/all_to_all | solution.py:414
  103.3 5.9 %weigh.1 = (f32[8,128]{1,0:T(8,128)}, f32[384,128]{1,0:T(8,128)}) custom-call(s32[1]{0:T(128)} %bitcast.core_ref, f32[16,16,128]{2,1,0:T(8,128)} %all_to_all.25.parts_ref, f32[4,8,4,8,8,128]{5,4,3,2,1,0:T(8,128)} %get-tuple-element.9.unit_ref, f32[2,6,8,8,128]{4,3,2,1,0:T(8,128)} %get-tuple-element.10.tgt_ref, ...), custom_call_target="tpu_custom_call" | custom-call | tf_op jit(solution)/shard_map/weigh/pallas_call | solution.py:368
  109.2 0.9 reshape.26
  110.2 16.1 %all_to_all.26 = f32[32,12,128]{2,1,0:T(8,128)S(1)} all-to-all(f32[32,12,128]{2,1,0:T(8,128)S(1)} %reshape.26), channel_id=1, replica_groups={{0,16,32,48,64,80,96,112,128,144,160,176,192,208,224,240,256,272,288,30..., dimensions={0} | all-to-all | bytes 393216 | tf_op jit(solution)/shard_map/all_to_all | solution.py:418
  126.4 18.4 %all_to_all.27 = f32[32,12,128]{2,1,0:T(8,128)S(1)} all-to-all(f32[32,12,128]{2,1,0:T(8,128)S(1)} %broadcast_in_dim.28), channel_id=1, replica_groups={{0,16,32,48,64,80,96,112,128,144,160,176,192,208,224,240,256,272,288,30..., dimensions={0} | all-to-all | bytes 393216 | tf_op jit(solution)/shard_map/all_to_all | solution.py:422
  144.7 0.1 copy.27
  144.8 5.1 %collective-permute-start.1 = (f32[32,12,128]{2,0,1:T(8,128)S(1)}, f32[32,12,128]{2,0,1:T(8,128)S(1)}, u32[]{:S(2)}, u32[]{:S(2)}) collective-permute-start(f32[32,12,128]{2,0,1:T(8,128)S(1)} %copy.27), channel_id=1, source_target_pairs={{0,8},{8,0},{16,24},{24,16},{32,40},{40,32},{48,56},{56,48},{64,72... | collective-permute-start | bytes 589832 | tf_op jit(solution)/shard_map/ppermute | solution.py:426
  149.9 1.0 collective-permute-done.1
  150.9 0.1 broadcast_select_fusion.1
  151.0 0.1 maximum_bitcast_fusion
  151.1 0.8 reshape.27
  (6 shorter events, 0.1 us)
Async XLA Ops:
  2.4 30.8 %all-to-all-start = ((f32[64,3,128]{2,1,0:T(4,128)}), f32[64,3,128]{2,1,0:T(4,128)S(1)}, u32[]{:S(2)}, u32[]{:S(2)}) async-start(f32[64,3,128]{2,1,0:T(4,128)} %copy.23), calls=%async_computation | async-start | bytes 262144 | tf_op jit(solution)/shard_map/all_to_all | solution.py:402
  33.9 20.2 %all-to-all-start.1 = ((f32[32,12,128]{2,1,0:T(8,128)}), f32[32,12,128]{2,1,0:T(8,128)S(1)}, u32[]{:S(2)}, u32[]{:S(2)}) async-start(f32[32,12,128]{2,1,0:T(8,128)} %broadcast_in_dim.25), calls=%async_computation.1 | async-start | bytes 524288 | tf_op jit(solution)/shard_map/all_to_all | solution.py:407
  42.7 12.1 %copy-start = (f32[8,3,1024]{2,1,0:T(4,128)}, f32[8,3,1024]{2,1,0:T(4,128)S(1)}, u32[]{:S(2)}) copy-start(f32[8,3,1024]{2,1,0:T(4,128)S(1)} %copy.24.own_ref) | copy-start | bytes 294916
  42.7 12.1 %collective-permute-start = (f32[8,3,1024]{2,1,0:T(4,128)S(1)}, f32[8,3,1024]{2,1,0:T(4,128)S(1)}, u32[]{:S(2)}, u32[]{:S(2)}) collective-permute-start(f32[8,3,1024]{2,1,0:T(4,128)S(1)} %copy.24.own_ref), channel_id=1, source_target_pairs={{0,8},{8,0},{16,24},{24,16},{32,40},{40,32},{48,56},{56,48},{64,72... | collective-permute-start | bytes 294920 | tf_op jit(solution)/shard_map/ppermute | solution.py:399
  54.8 0.7 copy-start.1
  144.8 6.1 %collective-permute-start.1 = (f32[32,12,128]{2,0,1:T(8,128)S(1)}, f32[32,12,128]{2,0,1:T(8,128)S(1)}, u32[]{:S(2)}, u32[]{:S(2)}) collective-permute-start(f32[32,12,128]{2,0,1:T(8,128)S(1)} %copy.27), channel_id=1, source_target_pairs={{0,8},{8,0},{16,24},{24,16},{32,40},{40,32},{48,56},{56,48},{64,72... | collective-permute-start | bytes 589832 | tf_op jit(solution)/shard_map/ppermute | solution.py:426

commit v2 on v1

v2 whole, which is shorter than its diff:
```python
import functools

import jax
import jax.numpy as jnp
from jax import lax
from jax.experimental import pallas as pl
from jax.experimental.pallas import tpu as pltpu
from jax.sharding import PartitionSpec as P

LANES = 128
ROWS = 8
PIX = 1024
CH = 3
ALPHA = 1.6 / 9.0
W = 1.6
BIAS = 0.1
LOSS = 64.0
Q = 2.0 / 3.141592653589793

WIDE = (0.9999998602381658, 0.16669029577848243, 0.07435772061999424,
        0.05091170352566525, 0.0038116604731453715, 0.0690369823030177)
NARROW = (1.000000019010712, 0.16666188274704566, 0.07519150147740127, 0.04200062838628592,
          0.04465464851544397)


def half_arcsin(z, o, r, coefficients):
    y = z * lax.rsqrt(1.0 + o * r)
    y2 = y * y
    scaled = [2.0**0.5 * ALPHA * Q * c * 0.5**k for k, c in enumerate(coefficients)]
    total = scaled[-1]
    for c in scaled[-2::-1]:
        total = total * y2 + c
    return y * total


def lane_masks():
    lane = lax.broadcasted_iota(jnp.int32, (8, LANES), 1)
    x = lane % 32
    return (x > 0, x < 31, lane >= 32, lane < 96, [lane // 32 == k for k in range(1, 4)])


def box(v, masks):
    left, right, above, below, _ = masks
    r = []
    for a in v:
        r.append(
            a
            + jnp.where(left, pltpu.roll(a, 1, 1), 0.0)
            + jnp.where(right, pltpu.roll(a, LANES - 1, 1), 0.0)
        )
    first = jnp.where(above, pltpu.roll(r[7], 32, 1), 0.0)
    last = jnp.where(below, pltpu.roll(r[0], LANES - 32, 1), 0.0)
    r = [first] + r + [last]
    out = []
    for k in range(0, 8, 2):
        pair = r[k + 1] + r[k + 2]
        out.append(r[k] + pair)
        out.append(pair + r[k + 3])
    return out


def interleave(nat, masks):
    groups = masks[4]
    out = []
    for r in range(8):
        m, q = r // 4, r % 4
        v = None
        for y in range(4):
            a = nat[2 * y + m]
            shift = (32 * (y - q)) % LANES
            a = a if shift == 0 else pltpu.roll(a, shift, 1)
            v = a if v is None else jnp.where(groups[y - 1], a, v)
        out.append(v)
    return out


def deinterleave(v, masks):
    groups = masks[4]
    out = []
    for m in range(8):
        y, h = m // 2, m % 2
        o = None
        for q in range(4):
            a = v[4 * h + q]
            shift = (32 * (q - y)) % LANES
            a = a if shift == 0 else pltpu.roll(a, shift, 1)
            o = a if o is None else jnp.where(groups[q - 1], a, o)
        out.append(o)
    return out


def chain(channels, masks):
    squares = [a * a + b * b + d * d for a, b, d in zip(*channels)]
    n = [(ALPHA / CH) * a + BIAS for a in box(squares, masks)]
    factors, slopes = [], []
    for h in range(3):
        b = [lax.rsqrt(1.0 + 2.0 * a) for a in n]
        factors.append(b)
        if h < 2:
            act = []
            slope = []
            for a, bb in zip(n, b):
                inv = bb * bb
                z = 2.0 * a * inv
                rr = lax.rsqrt(1.0 + 4.0 * a)
                o = (1.0 + 4.0 * a) * (inv * inv)
                r = (1.0 + 2.0 * a) * rr
                act.append(half_arcsin(z, o, r, WIDE if h == 0 else NARROW))
                slope.append(2.0 * Q * inv * rr)
            slopes.append(slope)
            n = [a + BIAS for a in box(act, masks)]
    return factors, slopes


def target_kernel(images_ref, out_ref):
    masks = lane_masks()
    chans = []
    for ch in range(CH):
        nat = [images_ref[:, ch, m * LANES:(m + 1) * LANES] for m in range(8)]
        chans.append(interleave(nat, masks))
    factors, _ = chain(chans, masks)
    for r in range(8):
        for ch in range(CH):
            out_ref[ch, r] = (ALPHA / CH) * chans[ch][r]
        for h in range(3):
            out_ref[3 + h, r] = 2.0 * factors[h][r]


def coef_rows(coef_ref, core, g):
    both = []
    for b in range(2):
        rows = coef_ref[2 * g + b]
        pick = [jnp.where(core == 0, rows[2 * k:2 * k + 1], rows[2 * k + 1:2 * k + 2]) for k in range(4)]
        both.extend(pick)
    rows = jnp.concatenate(both, axis=0)
    return jnp.concatenate([rows, jnp.zeros((8, LANES - rows.shape[1]), jnp.float32)], axis=1)


def pair_chain(tgt, sup, masks, put):
    R = range(8)

    def layer(h, S, theta):
        p2 = [tgt(3 + h, r) * sup(3 + h, r) for r in R]
        z = [p * s for p, s in zip(p2, S)]
        o = [1.0 - a * a for a in z]
        rt = [lax.rsqrt(a) for a in o]
        act = [half_arcsin(a, b, c, WIDE if h == 0 else NARROW) for a, b, c in zip(z, o, rt)]
        u = [(ALPHA * Q) * a for a in rt]
        D = [a * b for a, b in zip(p2, u)]
        f = [a * b * (c * c) for a, b, c in zip(p2, theta, rt)]
        return z, act, u, D, f

    cross = [tgt(0, r) * sup(0, r) + tgt(1, r) * sup(1, r) + tgt(2, r) * sup(2, r) for r in R]
    yield
    S1 = [a + BIAS for a in box(cross, masks)]
    yield
    z1, A1, u1, D1, f1 = layer(0, S1, S1)
    yield
    back = box([x * y for x, y in zip(S1, D1)], masks)
    S2 = [a + BIAS for a in box(A1, masks)]
    T2 = [s + a for s, a in zip(S2, back)]
    yield
    z2, A2, u2, D2, f2 = layer(1, S2, T2)
    yield
    back = box([x * y for x, y in zip(T2, D2)], masks)
    S3 = [a + BIAS for a in box(A2, masks)]
    T3 = [s + a for s, a in zip(S3, back)]
    yield
    z3, A3, u3, D3, f3 = layer(2, S3, T3)
    yield
    gp = box(D3, masks)
    gs = [D3[r] * (2.0 + z3[r] * f3[r]) for r in R]
    for r in R:
        put(3, r, u3[r] * (z3[r] + f3[r]))
    ga = box(gs, masks)
    terms = [A3[r] + T3[r] * D3[r] for r in R]
    while len(terms) > 1:
        terms = [a + b for a, b in zip(terms[::2], terms[1::2])]
    entry = jnp.sum(terms[0], axis=1, keepdims=True) * (W / PIX / ALPHA) + BIAS
    yield
    gt, gs = [], []
    for r in R:
        e = gp[r] * f2[r]
        put(2, r, u2[r] * (z2[r] * ga[r] + e))
        gt.append(gp[r] * D2[r])
        gs.append(D2[r] * (ga[r] + gp[r] + z2[r] * e))
    gp = box(gt, masks)
    ga = box(gs, masks)
    yield
    gs = []
    for r in R:
        e = gp[r] * f1[r]
        put(1, r, u1[r] * (z1[r] * ga[r] + e))
        gs.append(D1[r] * (ga[r] + gp[r] + z1[r] * e))
    gx = box(gs, masks)
    for r in R:
        put(0, r, gx[r])
    yield entry


def main_kernel(core_ref, own_ref, other_ref, rows_ref, coef_ref, label_ref,
                parts_ref, unit_ref, sup_ref, kt_ref):
    masks = lane_masks()
    core = core_ref[0]
    step = pl.program_id(0)

    @pl.when(step == 0)
    def _():
        for g in range(2):
            chans = []
            for ch in range(CH):
                nat = []
                for m in range(8):
                    pieces = [
                        rows_ref[pl.ds(m * 48 + (2 * g + b) * 3 + ch, 4, stride=12), :]
                        for b in range(2)
                    ]
                    nat.append(jnp.concatenate(pieces, axis=0))
                chans.append(interleave(nat, masks))
            factors, slopes = chain(chans, masks)
            for r in range(8):
                for ch in range(CH):
                    sup_ref[g, ch, r] = chans[ch][r]
                for h in range(3):
                    sup_ref[g, 3 + h, r] = factors[h][r]
                for h in range(2):
                    sup_ref[g, 6 + h, r] = slopes[h][r]
        kt_ref[...] = jnp.zeros_like(kt_ref)

    g = step // 2
    lane = lax.broadcasted_iota(jnp.int32, (8, LANES), 1)

    def pair(i2, carry):
        def start(i, half, ref):
            t = (step % 2) * 4 + i

            def tgt(k, r):
                return jnp.broadcast_to(ref[k, r, pl.ds(t, 1), :], (8, LANES))

            def sup(k, r):
                return sup_ref[g, k, r]

            def put(k, r, value):
                unit_ref[0, i, half, k, r] = value

            return pair_chain(tgt, sup, masks, put)

        entries = None
        chains = [start(2 * i2 + j, half, ref) for j in range(2) for half, ref in enumerate((own_ref, other_ref))]
        for entries in zip(*chains):
            pass
        kt = kt_ref[g]
        for j in range(2):
            for half in range(2):
                kt = jnp.where(lane == 8 * half + (step % 2) * 4 + 2 * i2 + j, entries[2 * j + half], kt)
        kt_ref[g] = kt
        return carry

    lax.fori_loop(0, 2, pair, 0)

    @pl.when(step == 3)
    def _():
        part = None
        for g2 in range(2):
            term = lax.dot_general(
                kt_ref[g2], coef_rows(coef_ref, core, g2), (((0,), (0,)), ((), ())),
                precision=lax.Precision.HIGHEST, preferred_element_type=jnp.float32,
            )
            part = term if part is None else part + term
        own, other = part[0:8], part[8:16]
        own = jnp.where(lane == LANES - 1, label_ref[...], own)
        for peer in range(16):
            parts_ref[peer, pl.ds(pl.multiple_of(core * 8, 8), 8), :] = own
            parts_ref[peer, pl.ds(pl.multiple_of((1 - core) * 8, 8), 8), :] = other


def weigh_kernel(core_ref, parts_ref, unit_ref, own_ref, other_ref, sup_ref, coef_ref,
                 pred_ref, grad_ref, weight_ref, acc_ref):
    masks = lane_masks()
    core = core_ref[0]
    step = pl.program_id(0)
    lane = lax.broadcasted_iota(jnp.int32, (8, LANES), 1)
    classes = coef_ref.shape[2]

    @pl.when(step == 0)
    def _():
        errs = []
        for k, start in enumerate((core * 8, (1 - core) * 8)):
            start = pl.multiple_of(start, 8)
            vs = [parts_ref[peer, pl.ds(start, 8), :] for peer in range(16)]
            while len(vs) > 1:
                vs = [a + b for a, b in zip(vs[::2], vs[1::2])]
            v = vs[0]
            label = v[:, LANES - 1:LANES]
            onehot = jnp.where(lane.astype(jnp.float32) == label, 1.0, 0.0)
            if k == 0:
                pred_ref[...] = v
            errs.append(jnp.where(lane < classes, LOSS * (v - onehot), 0.0))
        err = jnp.concatenate(errs, axis=0)
        for g in range(2):
            wt = lax.dot_general(
                coef_rows(coef_ref, core, g), err, (((1,), (1,)), ((), ())),
                precision=lax.Precision.HIGHEST, preferred_element_type=jnp.float32,
            ) * (W / PIX / ALPHA)
            for t in range(16):
                weight_ref[g, t] = jnp.broadcast_to(wt[:, t:t + 1], (8, LANES))

    g = step // 2
    part = step % 2
    for r in range(8):
        acc = [None] * 6
        for i in range(4):
            for half, ref in enumerate((own_ref, other_ref)):
                t = part * 4 + i
                w = weight_ref[g, half * 8 + t]
                x = w * unit_ref[0, i, half, 0, r]
                terms = [
                    x * jnp.broadcast_to(ref[ch, r, pl.ds(t, 1), :], (8, LANES)) for ch in range(CH)
                ] + [w * unit_ref[0, i, half, 1 + h, r] for h in range(3)]
                acc = [b if a is None else a + b for a, b in zip(acc, terms)]
        for k in range(6):
            acc_ref[part, k, r] = acc[k]

    @pl.when(part == 1)
    def _():
        R = range(8)

        def variance(h):
            return [
                -(sup_ref[g, 3 + h, r] * sup_ref[g, 3 + h, r])
                * (acc_ref[0, 3 + h, r] + acc_ref[1, 3 + h, r])
                for r in R
            ]

        gn = variance(2)
        for h in (1, 0):
            back = box(gn, masks)
            own = variance(h)
            gn = [own[r] + ALPHA * back[r] * sup_ref[g, 6 + h, r] for r in R]
        back = box(gn, masks)
        for ch in range(CH):
            v = [
                acc_ref[0, ch, r] + acc_ref[1, ch, r]
                + (2.0 * ALPHA / CH) * sup_ref[g, ch, r] * back[r]
                for r in R
            ]
            nat = deinterleave(v, masks)
            for m in range(8):
                for b in range(2):
                    grad_ref[pl.ds(m * 48 + (2 * g + b) * 3 + ch, 4, stride=12), :] = nat[m][4 * b:4 * b + 4]


VMEM = pltpu.MemorySpace.VMEM
SMEM = pltpu.MemorySpace.SMEM


def whole(shape):
    return pl.BlockSpec(shape, lambda i: (0,) * len(shape))


def target_call(images):
    return pl.pallas_call(
        target_kernel,
        out_shape=jax.ShapeDtypeStruct((6, 8, 8, LANES), jnp.float32),
        name="targets",
    )(images)


UNIT = (4, 4, 2, 4, 8, 8, LANES)


def main_call(core, own, other, rows, coef, label):
    f32 = jnp.float32
    return pl.pallas_call(
        main_kernel,
        grid=(4,),
        in_specs=[
            pl.BlockSpec(memory_space=SMEM),
            whole((6, 8, 8, LANES)), whole((6, 8, 8, LANES)), whole((384, LANES)),
            whole(coef.shape), whole((8, 1)),
        ],
        out_specs=[
            whole((16, 16, LANES)),
            pl.BlockSpec((1,) + UNIT[1:], lambda i: (i,) + (0,) * 6),
            whole((2, 8, 8, 8, LANES)),
        ],
        out_shape=[
            jax.ShapeDtypeStruct((16, 16, LANES), f32),
            jax.ShapeDtypeStruct(UNIT, f32),
            jax.ShapeDtypeStruct((2, 8, 8, 8, LANES), f32),
        ],
        scratch_shapes=[pltpu.VMEM((2, 8, LANES), f32)],
        name="pairs",
    )(core, own, other, rows, coef, label)


def weigh_call(core, parts, unit, own, other, sup, coef):
    f32 = jnp.float32
    return pl.pallas_call(
        weigh_kernel,
        grid=(4,),
        in_specs=[
            pl.BlockSpec(memory_space=SMEM),
            whole((16, 16, LANES)),
            pl.BlockSpec((1,) + UNIT[1:], lambda i: (i,) + (0,) * 6),
            whole((6, 8, 8, LANES)), whole((6, 8, 8, LANES)),
            whole((2, 8, 8, 8, LANES)),
            whole(coef.shape),
        ],
        out_specs=[whole((8, LANES)), whole((384, LANES))],
        out_shape=[
            jax.ShapeDtypeStruct((8, LANES), f32),
            jax.ShapeDtypeStruct((384, LANES), f32),
        ],
        scratch_shapes=[pltpu.VMEM((2, 16, 8, LANES), f32), pltpu.VMEM((2, 6, 8, 8, LANES), f32)],
        name="weigh",
    )(core, parts, unit, own, other, sup, coef)


def local(tgt_n, sup_n, targets, labels, support_slots, block_owner, dual_coeffs):
    blocks = dual_coeffs.shape[0]
    classes = dual_coeffs.shape[2]
    index = lax.axis_index("tgt")
    core = (index % 2)[None].astype(jnp.int32)
    partner = [(t, t ^ 1) for t in range(tgt_n)]
    planes = [[t for t in range(tgt_n) if t % 2 == c] for c in range(2)]
    sets = [
        [t * sup_n + s for t in (2 * k, 2 * k + 1) for s in range(sup_n)] for k in range(tgt_n // 2)
    ]
    slot = support_slots[0].reshape(8, CH, 8, LANES)
    slot = slot.transpose(2, 0, 1, 3).reshape(tgt_n, CH, LANES)
    got = lax.all_to_all(slot, "tgt", 0, 0, tiled=True)
    own = target_call(targets)
    other = lax.ppermute(own, "tgt", partner)
    mine = jnp.concatenate(
        [lax.dynamic_slice_in_dim(got, block_owner[b], 1, 0) for b in range(blocks)], axis=0
    ).reshape(1, blocks * CH, LANES)
    half_n = tgt_n // 2
    rows = lax.all_to_all(
        jnp.broadcast_to(mine, (half_n, blocks * CH, LANES)), "tgt", 0, 0,
        axis_index_groups=planes, tiled=True,
    ).reshape(half_n * blocks * CH, LANES)
    first = lax.axis_index("sup") == 0
    label = jnp.where(first, labels.astype(jnp.float32), 0.0)[:, None]
    parts, unit, sup = main_call(core, own, other, rows, dual_coeffs, label)
    parts = lax.all_to_all(
        parts, ("tgt", "sup"), 0, 0, axis_index_groups=sets, tiled=True
    )
    pred, grad = weigh_call(core, parts, unit, own, other, sup, dual_coeffs)
    grad = lax.all_to_all(
        grad.reshape(half_n, blocks * CH, LANES), "tgt", 0, 0, axis_index_groups=planes, tiled=True
    )
    piece = jnp.sum(grad, axis=0, keepdims=True)
    full = lax.all_to_all(
        jnp.broadcast_to(piece, (half_n, blocks * CH, LANES)), "tgt", 0, 0,
        axis_index_groups=planes, tiled=True,
    )
    theirs = lax.ppermute(full, "tgt", partner)
    even = jnp.where(core[0] == 0, full, theirs)
    odd = jnp.where(core[0] == 0, theirs, full)
    both = jnp.stack([even, odd]).reshape(2, 8, 4, blocks, CH, LANES)
    out = both.transpose(3, 2, 0, 4, 1, 5).reshape(blocks, 8, CH, PIX)
    return pred[:, :classes], out


def solution(mesh):
    return jax.shard_map(
        functools.partial(local, mesh.shape["tgt"], mesh.shape["sup"]),
        mesh=mesh,
        in_specs=(
            P("tgt", None, None),
            P("tgt"),
            P("tgt", "sup", None, None),
            P(),
            P(None, "sup", None),
        ),
        out_specs=(P("tgt", None), P(None, "sup", None, None)),
        check_vma=False,
    )
```

time: 153 us -> 130 us (0.85)
  Pallas kernels: 40.9 us -> 20.7 us
  waiting for transfers between devices: 12.5 us -> 9.73 us
    pallas_call x1, Pallas kernels: 35 us -> 12.9 us  [main_call(): pl.pallas_call(main_kernel, grid=(4,), in_specs=[pl.BlockSpec(memory_spac...]
    all_to_all x1, waiting for transfers between devices: 7.44 us -> 4.6 us  [local(): lax.all_to_all(jnp.broadcast_to(mine, (half_n, blocks * CH, LANES)), 'tgt...]
    pallas_call x0 -> x1, Pallas kernels: none -> 2.21 us  [target_call(): pl.pallas_call(target_kernel, out_shape=jax.ShapeDtypeStruct((6, 8, 8, LA...]
    transpose x1 -> x2, local copies, waits for them, and re-layouts: 0.03 us -> 1.64 us  [the longest x1 1.62 us: local(): slot = slot.transpose(2, 0, 1, 3).reshape(tgt_n, CH, LANES)]
  transfers between devices with their start and end apart: 4 -> 4, of which waited for: 3 -> 3; matrix products, arithmetic and copies ran while one was open for 3% -> 4% of each run, Pallas kernels for 0% -> 2%
where the time goes in v2:
time: 130 us
  blocking collectives  47.7 us (37%)
  starting transfers between devices  33.1 us (25%)
  Pallas kernels  20.7 us (16%)
  waiting for transfers between devices  9.73 us (7%)
  local copies, waits for them, and re-layouts  9.33 us (7%)
  between operations  8.3 us (6%)
    all_to_all x1, blocking collectives, local(): lax.all_to_all(jnp.broadcast_to(piece, (half_n, blocks * CH, LANES)), 'tg...  18.3 us
    all_to_all x1, starting transfers between devices, local(): got = lax.all_to_all(slot, 'tgt', 0, 0, tiled=True)  17.6 us
    all_to_all x1, blocking collectives, local(): lax.all_to_all(grad.reshape(half_n, blocks * CH, LANES), 'tgt', 0, 0, axi...  16.4 us
    pallas_call x1, Pallas kernels, main_call(): pl.pallas_call(main_kernel, grid=(4,), in_specs=[pl.BlockSpec(memory_spac...  12.9 us
    all_to_all x1, blocking collectives, local(): lax.all_to_all(parts, ('tgt', 'sup'), 0, 0, axis_index_groups=sets, tiled...  12.9 us
    all_to_all x1, starting transfers between devices, local(): lax.all_to_all(jnp.broadcast_to(mine, (half_n, blocks * CH, LANES)), 'tgt...  7.81 us
    pallas_call x1, Pallas kernels, weigh_call(): pl.pallas_call(weigh_kernel, grid=(4,), in_specs=[pl.BlockSpec(memory_spa...  5.54 us
    ppermute x1, starting transfers between devices, local(): theirs = lax.ppermute(full, 'tgt', partner)  5.07 us
  transfers between devices with their start and end apart: 4, of which 3 were waited for; matrix products, arithmetic and copies ran while one was open for 4% of the time, Pallas kernels for 2%

profile of v2, /device:TPU:1, one launch (start us, length us, event | category | flops | bytes accessed | tf_op | source)
XLA Modules:
  0.0 129.7 jit_solution(15647942826676732486)
XLA Ops:
  0.6 1.6 %copy.18 = f32[8,8,3,128]{3,2,1,0:T(4,128)} copy(f32[8,8,3,128]{3,1,0,2:T(8,128)} %bitcast.22) | data formatting | bytes 196608 | tf_op jit(solution)/shard_map/transpose | solution.py:431
  2.2 17.6 %all-to-all-start = ((f32[64,3,128]{2,1,0:T(4,128)}), f32[64,3,128]{2,1,0:T(4,128)S(1)}, u32[]{:S(2)}, u32[]{:S(2)}) async-start(f32[64,3,128]{2,1,0:T(4,128)} %bitcast.3), calls=%async_computation | async-start | bytes 262144 | tf_op jit(solution)/shard_map/all_to_all | solution.py:432
  19.9 1.5 %fusion.1 = (s32[1]{0:T(128)}, s32[1]{0:T(128)}, s32[1]{0:T(128)}, s32[1]{0:T(128)}) fusion(s32[4]{0:T(128)} %param.8), kind=kLoop, calls=%fused_computation.10 | loop fusion | bytes 32 | tf_op jit(solution)/shard_map/slice | solution.py:436
  28.9 4.1 %all-to-all-done = f32[64,3,128]{2,1,0:T(4,128)S(1)} async-done(((f32[64,3,128]{2,1,0:T(4,128)}), f32[64,3,128]{2,1,0:T(4,128)S(1)}, u32[]{:S(2)}, u32[]{:S(2)}) %all-to-all-start) | async-done | bytes 98336 | tf_op jit(solution)/shard_map/all_to_all | solution.py:432
  33.0 0.7 broadcast_in_dim.25
  33.7 7.8 %all-to-all-start.1 = ((f32[32,12,128]{2,1,0:T(8,128)}), f32[32,12,128]{2,1,0:T(8,128)S(1)}, u32[]{:S(2)}, u32[]{:S(2)}) async-start(f32[32,12,128]{2,1,0:T(8,128)} %broadcast_in_dim.25), calls=%async_computation.1 | async-start | bytes 524288 | tf_op jit(solution)/shard_map/all_to_all | solution.py:439
  41.6 1.6 %copy.17.images_ref = f32[8,3,1024]{2,1,0:T(4,128)} copy(f32[8,3,1024]{2,0,1:T(8,128)} %param.5) | data formatting | bytes 196608 | tf_op args[0]
  43.2 2.2 %targets.1.own_ref = f32[6,8,8,128]{3,2,1,0:T(8,128)} custom-call(f32[8,3,1024]{2,1,0:T(4,128)} %copy.17.images_ref), custom_call_target="tpu_custom_call" | custom-call | tf_op jit(solution)/shard_map/targets/pallas_call | solution.py:362
  45.4 2.6 %collective-permute-start = (f32[6,8,8,128]{3,2,1,0:T(8,128)}, f32[6,8,8,128]{3,2,1,0:T(8,128)S(1)}, u32[]{:S(2)}, u32[]{:S(2)}) collective-permute-start(f32[6,8,8,128]{3,2,1,0:T(8,128)} %targets.1.own_ref), channel_id=1, source_target_pairs={{0,8},{8,0},{16,24},{24,16},{32,40},{40,32},{48,56},{56,48},{64,72... | collective-permute-start | bytes 589832 | tf_op jit(solution)/shard_map/ppermute | solution.py:434
  48.0 0.7 fusion
  48.6 0.7 copy.19.label_ref
  49.3 4.6 %all-to-all-done.1 = f32[32,12,128]{2,1,0:T(8,128)S(1)} async-done(((f32[32,12,128]{2,1,0:T(8,128)}), f32[32,12,128]{2,1,0:T(8,128)S(1)}, u32[]{:S(2)}, u32[]{:S(2)}) %all-to-all-start.1) | async-done | bytes 196640 | tf_op jit(solution)/shard_map/all_to_all | solution.py:439
  53.9 0.7 reshape.25.rows_ref
  54.6 0.0 collective-permute-done.other_ref
  54.6 0.0 copy-start
  54.6 0.7 copy-done
  55.3 12.9 %pairs.1 = (f32[16,16,128]{2,1,0:T(8,128)}, f32[4,4,2,4,8,8,128]{6,5,4,3,2,1,0:T(8,128)}, f32[2,8,8,8,128]{4,3,2,1,0:T(8,128)}) custom-call(s32[1]{0:T(128)} %bitcast.core_ref, f32[6,8,8,128]{3,2,1,0:T(8,128)} %targets.1.own_ref, f32[6,8,8,128]{3,2,1,0:T(8,128)} %copy-done, f32[384,128]{1,0:T(8,128)} %reshape.25.rows_ref, f32[4,8,100]{2,1,0:T(8,128)} %coef_ref.3, ...), custom_call_target="tpu_custom_call" | custom-call | tf_op jit(solution)/shard_map/pairs/pallas_call | solution.py:374
  68.2 12.9 %all_to_all.25.parts_ref = f32[16,16,128]{2,1,0:T(8,128)} all-to-all(f32[16,16,128]{2,1,0:T(8,128)} %get-tuple-element.7), channel_id=1, replica_groups={{0,1,2,3,4,5,6,7,8,9,10,11,12,13,14,15},{16,17,18,19,20,21,22,23,24,25,..., dimensions={0} | all-to-all | bytes 262144 | tf_op jit(solution)/shard_map/all_to_all | solution.py:446
  81.1 5.5 %weigh.1 = (f32[8,128]{1,0:T(8,128)}, f32[384,128]{1,0:T(8,128)}) custom-call(s32[1]{0:T(128)} %bitcast.core_ref, f32[16,16,128]{2,1,0:T(8,128)} %all_to_all.25.parts_ref, f32[4,4,2,4,8,8,128]{6,5,4,3,2,1,0:T(8,128)} %get-tuple-element.8.unit_ref, f32[6,8,8,128]{3,2,1,0:T(8,128)} %targets.1.own_ref, f32[6,8,8,128]{3,2,1,0:T(8,128)} %copy-done, ...), custom_call_target="tpu_custom_call" | custom-call | tf_op jit(solution)/shard_map/weigh/pallas_call | solution.py:399
  86.6 0.9 reshape.26
  87.6 16.4 %all_to_all.26 = f32[32,12,128]{2,1,0:T(8,128)S(1)} all-to-all(f32[32,12,128]{2,1,0:T(8,128)S(1)} %reshape.26), channel_id=1, replica_groups={{0,16,32,48,64,80,96,112,128,144,160,176,192,208,224,240,256,272,288,30..., dimensions={0} | all-to-all | bytes 393216 | tf_op jit(solution)/shard_map/all_to_all | solution.py:450
  104.1 18.3 %all_to_all.27 = f32[32,12,128]{2,1,0:T(8,128)S(1)} all-to-all(f32[32,12,128]{2,1,0:T(8,128)S(1)} %broadcast_in_dim.28), channel_id=1, replica_groups={{0,16,32,48,64,80,96,112,128,144,160,176,192,208,224,240,256,272,288,30..., dimensions={0} | all-to-all | bytes 393216 | tf_op jit(solution)/shard_map/all_to_all | solution.py:454
  122.4 0.1 copy.21
  122.5 5.1 %collective-permute-start.1 = (f32[32,12,128]{2,0,1:T(8,128)S(1)}, f32[32,12,128]{2,0,1:T(8,128)S(1)}, u32[]{:S(2)}, u32[]{:S(2)}) collective-permute-start(f32[32,12,128]{2,0,1:T(8,128)S(1)} %copy.21), channel_id=1, source_target_pairs={{0,8},{8,0},{16,24},{24,16},{32,40},{40,32},{48,56},{56,48},{64,72... | collective-permute-start | bytes 589832 | tf_op jit(solution)/shard_map/ppermute | solution.py:458
  127.6 1.0 collective-permute-done.1
  128.6 0.1 broadcast_select_fusion.1
  128.7 0.1 maximum_bitcast_fusion
  128.9 0.8 reshape.27
  (6 shorter events, 0.1 us)
Async XLA Ops:
  2.2 30.8 %all-to-all-start = ((f32[64,3,128]{2,1,0:T(4,128)}), f32[64,3,128]{2,1,0:T(4,128)S(1)}, u32[]{:S(2)}, u32[]{:S(2)}) async-start(f32[64,3,128]{2,1,0:T(4,128)} %bitcast.3), calls=%async_computation | async-start | bytes 262144 | tf_op jit(solution)/shard_map/all_to_all | solution.py:432
  33.7 20.2 %all-to-all-start.1 = ((f32[32,12,128]{2,1,0:T(8,128)}), f32[32,12,128]{2,1,0:T(8,128)S(1)}, u32[]{:S(2)}, u32[]{:S(2)}) async-start(f32[32,12,128]{2,1,0:T(8,128)} %broadcast_in_dim.25), calls=%async_computation.1 | async-start | bytes 524288 | tf_op jit(solution)/shard_map/all_to_all | solution.py:439
  45.4 9.2 %collective-permute-start = (f32[6,8,8,128]{3,2,1,0:T(8,128)}, f32[6,8,8,128]{3,2,1,0:T(8,128)S(1)}, u32[]{:S(2)}, u32[]{:S(2)}) collective-permute-start(f32[6,8,8,128]{3,2,1,0:T(8,128)} %targets.1.own_ref), channel_id=1, source_target_pairs={{0,8},{8,0},{16,24},{24,16},{32,40},{40,32},{48,56},{56,48},{64,72... | collective-permute-start | bytes 589832 | tf_op jit(solution)/shard_map/ppermute | solution.py:434
  54.6 0.7 copy-start
  122.5 6.1 %collective-permute-start.1 = (f32[32,12,128]{2,0,1:T(8,128)S(1)}, f32[32,12,128]{2,0,1:T(8,128)S(1)}, u32[]{:S(2)}, u32[]{:S(2)}) collective-permute-start(f32[32,12,128]{2,0,1:T(8,128)S(1)} %copy.21), channel_id=1, source_target_pairs={{0,8},{8,0},{16,24},{24,16},{32,40},{40,32},{48,56},{56,48},{64,72... | collective-permute-start | bytes 589832 | tf_op jit(solution)/shard_map/ppermute | solution.py:458

commit v3 on v2

--- a/solution.py
+++ b/solution.py
@@ -112,7 +112,15 @@
     return factors, slopes
 
 
-def target_kernel(images_ref, out_ref):
+def slot_kernel(slot_ref, out_ref):
+    for ch in range(CH):
+        for m in range(8):
+            out_ref[pl.ds(m * 32 + ch, 8, stride=4), :] = slot_ref[ch, :, m * LANES:(m + 1) * LANES]
+    for m in range(8):
+        out_ref[pl.ds(m * 32 + CH, 8, stride=4), :] = jnp.zeros((8, LANES), jnp.float32)
+
+
+def target_kernel(core_ref, owner_ref, images_ref, coef_ref, out_ref, rows_ref, lanes_ref):
     masks = lane_masks()
     chans = []
     for ch in range(CH):
@@ -124,6 +132,10 @@
             out_ref[ch, r] = (ALPHA / CH) * chans[ch][r]
         for h in range(3):
             out_ref[3 + h, r] = 2.0 * factors[h][r]
+    for g in range(2):
+        rows_ref[g] = coef_rows(coef_ref, core_ref[0], g)
+    for b in range(owner_ref.shape[0]):
+        lanes_ref[b:b + 1, :] = jnp.full((1, LANES), owner_ref[b], jnp.int32)
 
 
 def coef_rows(coef_ref, core, g):
@@ -212,7 +224,7 @@
                 nat = []
                 for m in range(8):
                     pieces = [
-                        rows_ref[pl.ds(m * 48 + (2 * g + b) * 3 + ch, 4, stride=12), :]
+                        rows_ref[pl.ds(m * 48 + ch * 4 + 2 * g + b, 4, stride=12), :]
                         for b in range(2)
                     ]
                     nat.append(jnp.concatenate(pieces, axis=0))
@@ -241,7 +253,7 @@
                 return sup_ref[g, k, r]
 
             def put(k, r, value):
-                unit_ref[0, i, half, k, r] = value
+                unit_ref[step, i, half, k, r] = value
 
             return pair_chain(tgt, sup, masks, put)
 
@@ -263,7 +275,7 @@
         part = None
         for g2 in range(2):
             term = lax.dot_general(
-                kt_ref[g2], coef_rows(coef_ref, core, g2), (((0,), (0,)), ((), ())),
+                kt_ref[g2], coef_ref[g2], (((0,), (0,)), ((), ())),
                 precision=lax.Precision.HIGHEST, preferred_element_type=jnp.float32,
             )
             part = term if part is None else part + term
@@ -274,13 +286,12 @@
             parts_ref[peer, pl.ds(pl.multiple_of((1 - core) * 8, 8), 8), :] = other
 
 
-def weigh_kernel(core_ref, parts_ref, unit_ref, own_ref, other_ref, sup_ref, coef_ref,
+def weigh_kernel(classes, core_ref, parts_ref, unit_ref, own_ref, other_ref, sup_ref, coef_ref,
                  pred_ref, grad_ref, weight_ref, acc_ref):
     masks = lane_masks()
     core = core_ref[0]
     step = pl.program_id(0)
     lane = lax.broadcasted_iota(jnp.int32, (8, LANES), 1)
-    classes = coef_ref.shape[2]
 
     @pl.when(step == 0)
     def _():
@@ -299,7 +310,7 @@
         err = jnp.concatenate(errs, axis=0)
         for g in range(2):
             wt = lax.dot_general(
-                coef_rows(coef_ref, core, g), err, (((1,), (1,)), ((), ())),
+                coef_ref[g], err, (((1,), (1,)), ((), ())),
                 precision=lax.Precision.HIGHEST, preferred_element_type=jnp.float32,
             ) * (W / PIX / ALPHA)
             for t in range(16):
@@ -313,10 +324,10 @@
             for half, ref in enumerate((own_ref, other_ref)):
                 t = part * 4 + i
                 w = weight_ref[g, half * 8 + t]
-                x = w * unit_ref[0, i, half, 0, r]
+                x = w * unit_ref[step, i, half, 0, r]
                 terms = [
                     x * jnp.broadcast_to(ref[ch, r, pl.ds(t, 1), :], (8, LANES)) for ch in range(CH)
-                ] + [w * unit_ref[0, i, half, 1 + h, r] for h in range(3)]
+                ] + [w * unit_ref[step, i, half, 1 + h, r] for h in range(3)]
                 acc = [b if a is None else a + b for a, b in zip(acc, terms)]
         for k in range(6):
             acc_ref[part, k, r] = acc[k]
@@ -347,23 +358,62 @@
             nat = deinterleave(v, masks)
             for m in range(8):
                 for b in range(2):
-                    grad_ref[pl.ds(m * 48 + (2 * g + b) * 3 + ch, 4, stride=12), :] = nat[m][4 * b:4 * b + 4]
+                    grad_ref[pl.ds(m * 48 + ch * 4 + 2 * g + b, 4, stride=12), :] = nat[m][4 * b:4 * b + 4]
 
 
 VMEM = pltpu.MemorySpace.VMEM
 SMEM = pltpu.MemorySpace.SMEM
-
-
-def whole(shape):
-    return pl.BlockSpec(shape, lambda i: (0,) * len(shape))
-
-
-def target_call(images):
+FULL = pl.BlockSpec(memory_space=VMEM)
+PARAMS = pltpu.CompilerParams(vmem_limit_bytes=24 * 2**20)
+
+
+def slot_call(slot):
+    return pl.pallas_call(
+        slot_kernel,
+        in_specs=[FULL], out_specs=FULL,
+        out_shape=jax.ShapeDtypeStruct((256, LANES), jnp.float32),
+        compiler_params=PARAMS,
+        name="slot",
+    )(slot)
+
+
+def target_call(core, owner, images, coef):
+    f32 = jnp.float32
     return pl.pallas_call(
         target_kernel,
-        out_shape=jax.ShapeDtypeStruct((6, 8, 8, LANES), jnp.float32),
+        in_specs=[pl.BlockSpec(memory_space=SMEM)] * 2 + [FULL, FULL],
+        out_specs=[FULL] * 3,
+        out_shape=[
+            jax.ShapeDtypeStruct((6, 8, 8, LANES), f32),
+            jax.ShapeDtypeStruct((2, 8, LANES), f32),
+            jax.ShapeDtypeStruct((owner.shape[0], LANES), jnp.int32),
+        ],
+        compiler_params=PARAMS,
         name="targets",
-    )(images)
+    )(core, owner, images, coef)
+
+
+def pick_kernel(owner_ref, got_ref, out_ref):
+    blocks = [jnp.zeros(got_ref.shape[1:], jnp.float32)] * owner_ref.shape[0]
+    owners = [jnp.broadcast_to(owner_ref[b:b + 1, :], got_ref.shape[1:]) for b in range(len(blocks))]
+    for slot in range(got_ref.shape[0]):
+        v = got_ref[slot]
+        blocks = [jnp.where(o == slot, v, a) for o, a in zip(owners, blocks)]
+    piece = [v[ch:ch + 1] for ch in range(CH) for v in blocks]
+    twice = jnp.concatenate(piece + piece, axis=0)
+    for k in range(out_ref.shape[0] // twice.shape[0]):
+        out_ref[k * twice.shape[0]:(k + 1) * twice.shape[0], :] = twice
+
+
+def pick_call(owner, got, count):
+    return pl.pallas_call(
+        pick_kernel,
+        in_specs=[FULL, FULL],
+        out_specs=FULL,
+        out_shape=jax.ShapeDtypeStruct((count * CH * owner.shape[0], LANES), jnp.float32),
+        compiler_params=PARAMS,
+        name="pick",
+    )(owner, got)
 
 
 UNIT = (4, 4, 2, 4, 8, 8, LANES)
@@ -376,13 +426,13 @@
         grid=(4,),
         in_specs=[
             pl.BlockSpec(memory_space=SMEM),
-            whole((6, 8, 8, LANES)), whole((6, 8, 8, LANES)), whole((384, LANES)),
-            whole(coef.shape), whole((8, 1)),
+            FULL, FULL, FULL,
+            FULL, FULL,
         ],
         out_specs=[
-            whole((16, 16, LANES)),
-            pl.BlockSpec((1,) + UNIT[1:], lambda i: (i,) + (0,) * 6),
-            whole((2, 8, 8, 8, LANES)),
+            FULL,
+            FULL,
+            FULL,
         ],
         out_shape=[
             jax.ShapeDtypeStruct((16, 16, LANES), f32),
@@ -390,29 +440,31 @@
             jax.ShapeDtypeStruct((2, 8, 8, 8, LANES), f32),
         ],
         scratch_shapes=[pltpu.VMEM((2, 8, LANES), f32)],
+        compiler_params=PARAMS,
         name="pairs",
     )(core, own, other, rows, coef, label)
 
 
-def weigh_call(core, parts, unit, own, other, sup, coef):
+def weigh_call(classes, core, parts, unit, own, other, sup, coef):
     f32 = jnp.float32
     return pl.pallas_call(
-        weigh_kernel,
+        functools.partial(weigh_kernel, classes),
         grid=(4,),
         in_specs=[
             pl.BlockSpec(memory_space=SMEM),
-            whole((16, 16, LANES)),
-            pl.BlockSpec((1,) + UNIT[1:], lambda i: (i,) + (0,) * 6),
-            whole((6, 8, 8, LANES)), whole((6, 8, 8, LANES)),
-            whole((2, 8, 8, 8, LANES)),
-            whole(coef.shape),
+            FULL,
+            FULL,
+            FULL, FULL,
+            FULL,
+            FULL,
         ],
-        out_specs=[whole((8, LANES)), whole((384, LANES))],
+        out_specs=[FULL, FULL],
         out_shape=[
             jax.ShapeDtypeStruct((8, LANES), f32),
             jax.ShapeDtypeStruct((384, LANES), f32),
         ],
         scratch_shapes=[pltpu.VMEM((2, 16, 8, LANES), f32), pltpu.VMEM((2, 6, 8, 8, LANES), f32)],
+        compiler_params=PARAMS,
         name="weigh",
     )(core, parts, unit, own, other, sup, coef)
 
@@ -427,39 +479,36 @@
     sets = [
         [t * sup_n + s for t in (2 * k, 2 * k + 1) for s in range(sup_n)] for k in range(tgt_n // 2)
     ]
-    slot = support_slots[0].reshape(8, CH, 8, LANES)
-    slot = slot.transpose(2, 0, 1, 3).reshape(tgt_n, CH, LANES)
+    slot = slot_call(support_slots[0].transpose(1, 0, 2)).reshape(tgt_n, 4, LANES)
     got = lax.all_to_all(slot, "tgt", 0, 0, tiled=True)
-    own = target_call(targets)
+    own, coef, owner = target_call(core, block_owner, targets, dual_coeffs)
+    got, own, owner = lax.optimization_barrier((got, own, owner))
     other = lax.ppermute(own, "tgt", partner)
-    mine = jnp.concatenate(
-        [lax.dynamic_slice_in_dim(got, block_owner[b], 1, 0) for b in range(blocks)], axis=0
-    ).reshape(1, blocks * CH, LANES)
     half_n = tgt_n // 2
+    piece_shape = (half_n, CH, blocks, LANES)
     rows = lax.all_to_all(
-        jnp.broadcast_to(mine, (half_n, blocks * CH, LANES)), "tgt", 0, 0,
+        pick_call(owner, got, half_n).reshape(piece_shape), "tgt", 0, 0,
         axis_index_groups=planes, tiled=True,
     ).reshape(half_n * blocks * CH, LANES)
     first = lax.axis_index("sup") == 0
     label = jnp.where(first, labels.astype(jnp.float32), 0.0)[:, None]
-    parts, unit, sup = main_call(core, own, other, rows, dual_coeffs, label)
+    parts, unit, sup = main_call(core, own, other, rows, coef, label)
     parts = lax.all_to_all(
         parts, ("tgt", "sup"), 0, 0, axis_index_groups=sets, tiled=True
     )
-    pred, grad = weigh_call(core, parts, unit, own, other, sup, dual_coeffs)
+    pred, grad = weigh_call(classes, core, parts, unit, own, other, sup, coef)
     grad = lax.all_to_all(
-        grad.reshape(half_n, blocks * CH, LANES), "tgt", 0, 0, axis_index_groups=planes, tiled=True
+        grad.reshape(piece_shape), "tgt", 0, 0, axis_index_groups=planes, tiled=True
     )
     piece = jnp.sum(grad, axis=0, keepdims=True)
     full = lax.all_to_all(
-        jnp.broadcast_to(piece, (half_n, blocks * CH, LANES)), "tgt", 0, 0,
-        axis_index_groups=planes, tiled=True,
+        jnp.broadcast_to(piece, piece_shape), "tgt", 0, 0, axis_index_groups=planes, tiled=True
     )
     theirs = lax.ppermute(full, "tgt", partner)
     even = jnp.where(core[0] == 0, full, theirs)
     odd = jnp.where(core[0] == 0, theirs, full)
-    both = jnp.stack([even, odd]).reshape(2, 8, 4, blocks, CH, LANES)
-    out = both.transpose(3, 2, 0, 4, 1, 5).reshape(blocks, 8, CH, PIX)
+    both = jnp.stack([even, odd]).reshape(2, 8, 4, CH, blocks, LANES)
+    out = both.transpose(4, 2, 0, 3, 1, 5).reshape(blocks, 8, CH, PIX)
     return pred[:, :classes], out
 
 

time: 130 us -> 115 us (0.88)
  waiting for transfers between devices: 9.73 us -> 19.1 us
  between operations: 8.3 us -> 0.76 us
  local copies, waits for them, and re-layouts: 9.33 us -> 4.18 us
  starting transfers between devices: 33.1 us -> 28.2 us
  Pallas kernels: 20.7 us -> 15.8 us
  blocking collectives: 47.7 us -> 45.1 us
    all_to_all x1, waiting for transfers between devices: 4.08 us -> 9.6 us  [local(): got = lax.all_to_all(slot, 'tgt', 0, 0, tiled=True)]
    all_to_all x1, starting transfers between devices: 7.81 us -> 3.86 us  [local(): lax.all_to_all(pick_call(owner, got, half_n).reshape(piece_shape), 'tgt',...]
    all_to_all x1, waiting for transfers between devices: 4.6 us -> 8.1 us  [local(): lax.all_to_all(pick_call(owner, got, half_n).reshape(piece_shape), 'tgt',...]
    all_to_all x2, blocking collectives: 34.8 us -> 32.1 us  [the longest x1 16.8 us: local(): lax.all_to_all(jnp.broadcast_to(piece, piece_shape), 'tgt', 0, 0, axis_in...]
    pallas_call x1, Pallas kernels: 12.9 us -> 10.4 us  [main_call(): pl.pallas_call(main_kernel, grid=(4,), in_specs=[pl.BlockSpec(memory_spac...]
    pallas_call x2 -> x4, Pallas kernels: 7.76 us -> 5.36 us  [the longest x1 2.78 us: weigh_call(): pl.pallas_call(functools.partial(weigh_kernel, classes), grid=(4,), in_sp...]
    reshape x3 -> x1, local copies, waits for them, and re-layouts: 2.45 us -> 0.81 us  [local(): out = both.transpose(4, 2, 0, 3, 1, 5).reshape(blocks, 8, CH, PIX)]
    transpose x2 -> x1, local copies, waits for them, and re-layouts: 1.64 us -> 0.03 us  [local(): out = both.transpose(4, 2, 0, 3, 1, 5).reshape(blocks, 8, CH, PIX)]
  transfers between devices with their start and end apart: 4 -> 4, of which waited for: 3 -> 4; matrix products, arithmetic and copies ran while one was open for 4% -> 1% of each run, Pallas kernels for 2% -> 1%
where the time goes in v3:
time: 115 us; the launch traced here: 114 us
  blocking collectives  45.1 us (39%)
  starting transfers between devices  28.2 us (25%)
  waiting for transfers between devices  19.1 us (17%)
  Pallas kernels  15.8 us (14%)
  local copies, waits for them, and re-layouts  4.18 us (4%)
    all_to_all x1, starting transfers between devices, local(): got = lax.all_to_all(slot, 'tgt', 0, 0, tiled=True)  17.6 us
    all_to_all x1, blocking collectives, local(): lax.all_to_all(jnp.broadcast_to(piece, piece_shape), 'tgt', 0, 0, axis_in...  16.8 us
    all_to_all x1, blocking collectives, local(): lax.all_to_all(grad.reshape(piece_shape), 'tgt', 0, 0, axis_index_groups=...  15.2 us
    all_to_all x1, blocking collectives, local(): lax.all_to_all(parts, ('tgt', 'sup'), 0, 0, axis_index_groups=sets, tiled...  13 us
    pallas_call x1, Pallas kernels, main_call(): pl.pallas_call(main_kernel, grid=(4,), in_specs=[pl.BlockSpec(memory_spac...  10.4 us
    all_to_all x1, waiting for transfers between devices, local(): got = lax.all_to_all(slot, 'tgt', 0, 0, tiled=True)  9.6 us
    all_to_all x1, waiting for transfers between devices, local(): lax.all_to_all(pick_call(owner, got, half_n).reshape(piece_shape), 'tgt',...  8.1 us
    ppermute x1, starting transfers between devices, local(): theirs = lax.ppermute(full, 'tgt', partner)  4.43 us
  transfers between devices with their start and end apart: 4, of which 4 were waited for; matrix products, arithmetic and copies ran while one was open for 1% of the time, Pallas kernels for 1%

profile of v3, /device:TPU:1, one launch (start us, length us, event | category | flops | bytes accessed | tf_op | source)
XLA Modules:
  0.0 114.0 jit_solution(374495294668621713)
XLA Ops:
  0.6 0.0 copy-start
  0.6 0.9 copy-done
  1.5 0.7 slot.1
  2.2 17.6 %all-to-all-start = ((f32[64,4,128]{2,1,0:T(4,128)}), f32[64,4,128]{2,1,0:T(4,128)S(1)}, u32[]{:S(2)}, u32[]{:S(2)}) async-start(f32[64,4,128]{2,1,0:T(4,128)} %bitcast.3), calls=%async_computation | async-start | bytes 262144 | tf_op jit(solution)/shard_map/all_to_all | solution.py:483
  19.8 1.0 copy.14.images_ref
  20.8 0.0 copy-start.1
  20.8 0.7 copy-done.1
  21.5 0.0 copy-start.2
  21.5 0.7 copy-done.2
  22.2 1.2 %targets.1 = (f32[6,8,8,128]{3,2,1,0:T(8,128)S(1)}, f32[2,8,128]{2,1,0:T(8,128)S(1)}, s32[4,128]{1,0:T(4,128)S(1)}) custom-call(s32[1]{0:T(128)} %bitcast.core_ref, s32[4]{0:T(128)S(1)} %copy-done.2, f32[8,3,1024]{2,1,0:T(4,128)S(1)} %copy.14.images_ref, f32[4,8,100]{2,1,0:T(8,128)S(1)} %copy-done.1), custom_call_target="tpu_custom_call" | custom-call | tf_op jit(solution)/shard_map/targets/pallas_call | solution.py:382
  23.3 9.6 %all-to-all-done.got_ref = f32[64,4,128]{2,1,0:T(4,128)S(1)} async-done(((f32[64,4,128]{2,1,0:T(4,128)}), f32[64,4,128]{2,1,0:T(4,128)S(1)}, u32[]{:S(2)}, u32[]{:S(2)}) %all-to-all-start) | async-done | bytes 131104 | tf_op jit(solution)/shard_map/all_to_all | solution.py:483
  32.9 0.8 pick.1
  33.7 3.9 %all-to-all-start.1 = ((f32[32,3,4,128]{3,2,1,0:T(4,128)}), f32[32,3,4,128]{3,2,1,0:T(4,128)S(1)}, u32[]{:S(2)}, u32[]{:S(2)}) async-start(f32[32,3,4,128]{3,2,1,0:T(4,128)} %bitcast.4), calls=%async_computation.1 | async-start | bytes 393216 | tf_op jit(solution)/shard_map/all_to_all | solution.py:489
  37.6 2.3 %collective-permute-start = (f32[6,8,8,128]{3,2,1,0:T(8,128)S(1)}, f32[6,8,8,128]{3,2,1,0:T(8,128)S(1)}, u32[]{:S(2)}, u32[]{:S(2)}) collective-permute-start(f32[6,8,8,128]{3,2,1,0:T(8,128)S(1)} %get-tuple-element.15.own_ref), channel_id=1, source_target_pairs={{0,8},{8,0},{16,24},{24,16},{32,40},{40,32},{48,56},{56,48},{64,72... | collective-permute-start | bytes 589832 | tf_op jit(solution)/shard_map/ppermute | solution.py:486
  39.9 0.7 fusion
  40.6 0.1 copy.15.label_ref
  40.7 0.3 collective-permute-done.other_ref
  41.0 8.1 %all-to-all-done.1 = f32[32,3,4,128]{3,2,1,0:T(4,128)S(1)} async-done(((f32[32,3,4,128]{3,2,1,0:T(4,128)}), f32[32,3,4,128]{3,2,1,0:T(4,128)S(1)}, u32[]{:S(2)}, u32[]{:S(2)}) %all-to-all-start.1) | async-done | bytes 196640 | tf_op jit(solution)/shard_map/all_to_all | solution.py:489
  49.1 10.4 %pairs.1 = (f32[16,16,128]{2,1,0:T(8,128)S(1)}, f32[4,4,2,4,8,8,128]{6,5,4,3,2,1,0:T(8,128)S(1)}, f32[2,8,8,8,128]{4,3,2,1,0:T(8,128)S(1)}) custom-call(s32[1]{0:T(128)} %bitcast.core_ref, f32[6,8,8,128]{3,2,1,0:T(8,128)S(1)} %get-tuple-element.15.own_ref, f32[6,8,8,128]{3,2,1,0:T(8,128)S(1)} %collective-permute-done.other_ref, f32[384,128]{1,0:T(8,128)S(1)} %bitcast.19, ...), custom_call_target="tpu_custom_call" | custom-call | tf_op jit(solution)/shard_map/pairs/pallas_call | solution.py:424
  59.5 13.0 %all_to_all.25.parts_ref = f32[16,16,128]{2,1,0:T(8,128)S(1)} all-to-all(f32[16,16,128]{2,1,0:T(8,128)S(1)} %get-tuple-element.19), channel_id=1, replica_groups={{0,1,2,3,4,5,6,7,8,9,10,11,12,13,14,15},{16,17,18,19,20,21,22,23,24,25,..., dimensions={0} | all-to-all | bytes 262144 | tf_op jit(solution)/shard_map/all_to_all | solution.py:496
  72.5 2.8 %weigh.1 = (f32[8,128]{1,0:T(8,128)}, f32[384,128]{1,0:T(8,128)S(1)}) custom-call(s32[1]{0:T(128)} %bitcast.core_ref, f32[16,16,128]{2,1,0:T(8,128)S(1)} %all_to_all.25.parts_ref, f32[4,4,2,4,8,8,128]{6,5,4,3,2,1,0:T(8,128)S(1)} %get-tuple-element.20.unit_ref, f32[6,8,8,128]{3,2,1,0:T(8,128)S(1)} %get-tuple-element.15.own_ref, ...), custom_call_target="tpu_custom_call" | custom-call | tf_op jit(solution)/shard_map/weigh/pallas_call | solution.py:450
  75.3 15.2 %all_to_all.26 = f32[32,3,4,128]{3,2,1,0:T(4,128)S(1)} all-to-all(f32[32,3,4,128]{3,2,1,0:T(4,128)S(1)} %bitcast.20), channel_id=1, replica_groups={{0,16,32,48,64,80,96,112,128,144,160,176,192,208,224,240,256,272,288,30..., dimensions={0} | all-to-all | bytes 393216 | tf_op jit(solution)/shard_map/all_to_all | solution.py:500
  90.5 0.1 reduce_sum.9
  90.6 16.8 %all_to_all.27 = f32[32,3,4,128]{3,2,1,0:T(4,128)S(1)} all-to-all(f32[32,3,4,128]{3,2,1,0:T(4,128)S(1)} %broadcast_in_dim.19), channel_id=1, replica_groups={{0,16,32,48,64,80,96,112,128,144,160,176,192,208,224,240,256,272,288,30..., dimensions={0} | all-to-all | bytes 393216 | tf_op jit(solution)/shard_map/all_to_all | solution.py:504
  107.5 4.4 %collective-permute-start.1 = (f32[32,3,4,128]{3,0,2,1:T(8,128)S(1)}, f32[32,3,4,128]{3,0,2,1:T(8,128)S(1)}, u32[]{:S(2)}, u32[]{:S(2)}) collective-permute-start(f32[32,3,4,128]{3,0,2,1:T(8,128)S(1)} %copy.17), channel_id=1, source_target_pairs={{0,8},{8,0},{16,24},{24,16},{32,40},{40,32},{48,56},{56,48},{64,72... | collective-permute-start | bytes 589832 | tf_op jit(solution)/shard_map/ppermute | solution.py:507
  111.9 1.0 collective-permute-done.1
  113.0 0.1 maximum_bitcast_fusion
  113.2 0.8 reshape.29
  (4 shorter events, 0.1 us)
Async XLA Ops:
  0.6 0.9 copy-start
  2.2 30.8 %all-to-all-start = ((f32[64,4,128]{2,1,0:T(4,128)}), f32[64,4,128]{2,1,0:T(4,128)S(1)}, u32[]{:S(2)}, u32[]{:S(2)}) async-start(f32[64,4,128]{2,1,0:T(4,128)} %bitcast.3), calls=%async_computation | async-start | bytes 262144 | tf_op jit(solution)/shard_map/all_to_all | solution.py:483
  20.8 0.7 copy-start.1
  21.5 0.7 copy-start.2
  33.7 15.4 %all-to-all-start.1 = ((f32[32,3,4,128]{3,2,1,0:T(4,128)}), f32[32,3,4,128]{3,2,1,0:T(4,128)S(1)}, u32[]{:S(2)}, u32[]{:S(2)}) async-start(f32[32,3,4,128]{3,2,1,0:T(4,128)} %bitcast.4), calls=%async_computation.1 | async-start | bytes 393216 | tf_op jit(solution)/shard_map/all_to_all | solution.py:489
  37.6 3.4 %collective-permute-start = (f32[6,8,8,128]{3,2,1,0:T(8,128)S(1)}, f32[6,8,8,128]{3,2,1,0:T(8,128)S(1)}, u32[]{:S(2)}, u32[]{:S(2)}) collective-permute-start(f32[6,8,8,128]{3,2,1,0:T(8,128)S(1)} %get-tuple-element.15.own_ref), channel_id=1, source_target_pairs={{0,8},{8,0},{16,24},{24,16},{32,40},{40,32},{48,56},{56,48},{64,72... | collective-permute-start | bytes 589832 | tf_op jit(solution)/shard_map/ppermute | solution.py:486
  107.5 5.5 %collective-permute-start.1 = (f32[32,3,4,128]{3,0,2,1:T(8,128)S(1)}, f32[32,3,4,128]{3,0,2,1:T(8,128)S(1)}, u32[]{:S(2)}, u32[]{:S(2)}) collective-permute-start(f32[32,3,4,128]{3,0,2,1:T(8,128)S(1)} %copy.17), channel_id=1, source_target_pairs={{0,8},{8,0},{16,24},{24,16},{32,40},{40,32},{48,56},{56,48},{64,72... | collective-permute-start | bytes 589832 | tf_op jit(solution)/shard_map/ppermute | solution.py:507

commit v4 on v3

--- a/solution.py
+++ b/solution.py
@@ -8,7 +8,6 @@
 from jax.sharding import PartitionSpec as P
 
 LANES = 128
-ROWS = 8
 PIX = 1024
 CH = 3
 ALPHA = 1.6 / 9.0
@@ -26,7 +25,7 @@
 def half_arcsin(z, o, r, coefficients):
     y = z * lax.rsqrt(1.0 + o * r)
     y2 = y * y
-    scaled = [2.0**0.5 * ALPHA * Q * c * 0.5**k for k, c in enumerate(coefficients)]
+    scaled = [2.0**0.5 * c * 0.5**k for k, c in enumerate(coefficients)]
     total = scaled[-1]
     for c in scaled[-2::-1]:
         total = total * y2 + c
@@ -35,58 +34,48 @@
 
 def lane_masks():
     lane = lax.broadcasted_iota(jnp.int32, (8, LANES), 1)
-    x = lane % 32
-    return (x > 0, x < 31, lane >= 32, lane < 96, [lane // 32 == k for k in range(1, 4)])
+    edges = (lane % 8 > 0, lane % 8 < 7, lane >= 8, lane < LANES - 8)
+    k, h, c = lane // 16, lane // 8 % 2, lane % 8
+    tiled = (2 * h + k // 4) * 32 + 4 * c + k % 4
+    row, col = lane // 32, lane % 32
+    natural = ((row % 2) * 4 + col % 4) * 16 + (row // 2) * 8 + col // 4
+    swap = [(lane // (16 * bit)) % 2 == 1 for bit in (1, 2, 4)]
+    return edges, tiled, natural, swap
 
 
 def box(v, masks):
-    left, right, above, below, _ = masks
+    left, right, above, below = masks[0]
     r = []
-    for a in v:
-        r.append(
-            a
-            + jnp.where(left, pltpu.roll(a, 1, 1), 0.0)
-            + jnp.where(right, pltpu.roll(a, LANES - 1, 1), 0.0)
-        )
-    first = jnp.where(above, pltpu.roll(r[7], 32, 1), 0.0)
-    last = jnp.where(below, pltpu.roll(r[0], LANES - 32, 1), 0.0)
-    r = [first] + r + [last]
-    out = []
-    for k in range(0, 8, 2):
-        pair = r[k + 1] + r[k + 2]
-        out.append(r[k] + pair)
-        out.append(pair + r[k + 3])
+    for i in (0, 4):
+        c0, c1, c2, c3 = v[i:i + 4]
+        p, q = c0 + c1, c2 + c3
+        r.append(p + jnp.where(left, pltpu.roll(c3, 1, 1), 0.0))
+        r.append(p + c2)
+        r.append(c1 + q)
+        r.append(q + jnp.where(right, pltpu.roll(c0, LANES - 1, 1), 0.0))
+    out = [None] * 8
+    for j in range(4):
+        a, b = r[j], r[4 + j]
+        p = a + b
+        out[j] = p + jnp.where(above, pltpu.roll(b, 8, 1), 0.0)
+        out[4 + j] = p + jnp.where(below, pltpu.roll(a, LANES - 8, 1), 0.0)
     return out
 
 
+def exchange_blocks(v, masks):
+    v = list(v)
+    for n, bit in enumerate((1, 2, 4)):
+        odd = masks[3][n]
+        for i in range(8):
+            if not i & bit:
+                a, b = v[i], v[i + bit]
+                v[i] = jnp.where(odd, pltpu.roll(b, 16 * bit, 1), a)
+                v[i + bit] = jnp.where(odd, b, pltpu.roll(a, LANES - 16 * bit, 1))
+    return v
+
+
 def interleave(nat, masks):
-    groups = masks[4]
-    out = []
-    for r in range(8):
-        m, q = r // 4, r % 4
-        v = None
-        for y in range(4):
-            a = nat[2 * y + m]
-            shift = (32 * (y - q)) % LANES
-            a = a if shift == 0 else pltpu.roll(a, shift, 1)
-            v = a if v is None else jnp.where(groups[y - 1], a, v)
-        out.append(v)
-    return out
-
-
-def deinterleave(v, masks):
-    groups = masks[4]
-    out = []
-    for m in range(8):
-        y, h = m // 2, m % 2
-        o = None
-        for q in range(4):
-            a = v[4 * h + q]
-            shift = (32 * (q - y)) % LANES
-            a = a if shift == 0 else pltpu.roll(a, shift, 1)
-            o = a if o is None else jnp.where(groups[q - 1], a, o)
-        out.append(o)
-    return out
+    return exchange_blocks([jnp.take_along_axis(a, masks[1], axis=1) for a in nat], masks)
 
 
 def chain(channels, masks):
@@ -108,7 +97,7 @@
                 act.append(half_arcsin(z, o, r, WIDE if h == 0 else NARROW))
                 slope.append(2.0 * Q * inv * rr)
             slopes.append(slope)
-            n = [a + BIAS for a in box(act, masks)]
+            n = [(ALPHA * Q) * a + BIAS for a in box(act, masks)]
     return factors, slopes
 
 
@@ -129,9 +118,9 @@
     factors, _ = chain(chans, masks)
     for r in range(8):
         for ch in range(CH):
-            out_ref[ch, r] = (ALPHA / CH) * chans[ch][r]
+            out_ref[ch, r] = (1.0 / (CH * Q)) * chans[ch][r]
         for h in range(3):
-            out_ref[3 + h, r] = 2.0 * factors[h][r]
+            out_ref[3 + h, r] = (2.0 * ALPHA * Q) * factors[h][r]
     for g in range(2):
         rows_ref[g] = coef_rows(coef_ref, core_ref[0], g)
     for b in range(owner_ref.shape[0]):
@@ -157,25 +146,24 @@
         o = [1.0 - a * a for a in z]
         rt = [lax.rsqrt(a) for a in o]
         act = [half_arcsin(a, b, c, WIDE if h == 0 else NARROW) for a, b, c in zip(z, o, rt)]
-        u = [(ALPHA * Q) * a for a in rt]
-        D = [a * b for a, b in zip(p2, u)]
+        D = [a * b for a, b in zip(p2, rt)]
         f = [a * b * (c * c) for a, b, c in zip(p2, theta, rt)]
-        return z, act, u, D, f
+        return z, act, rt, D, f
 
     cross = [tgt(0, r) * sup(0, r) + tgt(1, r) * sup(1, r) + tgt(2, r) * sup(2, r) for r in R]
     yield
-    S1 = [a + BIAS for a in box(cross, masks)]
+    S1 = [a + BIAS / (ALPHA * Q) for a in box(cross, masks)]
     yield
     z1, A1, u1, D1, f1 = layer(0, S1, S1)
     yield
     back = box([x * y for x, y in zip(S1, D1)], masks)
-    S2 = [a + BIAS for a in box(A1, masks)]
+    S2 = [a + BIAS / (ALPHA * Q) for a in box(A1, masks)]
     T2 = [s + a for s, a in zip(S2, back)]
     yield
     z2, A2, u2, D2, f2 = layer(1, S2, T2)
     yield
     back = box([x * y for x, y in zip(T2, D2)], masks)
-    S3 = [a + BIAS for a in box(A2, masks)]
+    S3 = [a + BIAS / (ALPHA * Q) for a in box(A2, masks)]
     T3 = [s + a for s, a in zip(S3, back)]
     yield
     z3, A3, u3, D3, f3 = layer(2, S3, T3)
@@ -188,7 +176,7 @@
     terms = [A3[r] + T3[r] * D3[r] for r in R]
     while len(terms) > 1:
         terms = [a + b for a, b in zip(terms[::2], terms[1::2])]
-    entry = jnp.sum(terms[0], axis=1, keepdims=True) * (W / PIX / ALPHA) + BIAS
+    entry = jnp.sum(terms[0], axis=1, keepdims=True) * (W * Q / PIX) + BIAS
     yield
     gt, gs = [], []
     for r in R:
@@ -228,7 +216,7 @@
                         for b in range(2)
                     ]
                     nat.append(jnp.concatenate(pieces, axis=0))
-                chans.append(interleave(nat, masks))
+                chans.append(exchange_blocks(nat, masks))
             factors, slopes = chain(chans, masks)
             for r in range(8):
                 for ch in range(CH):
@@ -287,7 +275,7 @@
 
 
 def weigh_kernel(classes, core_ref, parts_ref, unit_ref, own_ref, other_ref, sup_ref, coef_ref,
-                 pred_ref, grad_ref, weight_ref, acc_ref):
+                 grad_ref, weight_ref, acc_ref):
     masks = lane_masks()
     core = core_ref[0]
     step = pl.program_id(0)
@@ -296,7 +284,7 @@
     @pl.when(step == 0)
     def _():
         errs = []
-        for k, start in enumerate((core * 8, (1 - core) * 8)):
+        for start in (core * 8, (1 - core) * 8):
             start = pl.multiple_of(start, 8)
             vs = [parts_ref[peer, pl.ds(start, 8), :] for peer in range(16)]
             while len(vs) > 1:
@@ -304,15 +292,13 @@
             v = vs[0]
             label = v[:, LANES - 1:LANES]
             onehot = jnp.where(lane.astype(jnp.float32) == label, 1.0, 0.0)
-            if k == 0:
-                pred_ref[...] = v
             errs.append(jnp.where(lane < classes, LOSS * (v - onehot), 0.0))
         err = jnp.concatenate(errs, axis=0)
         for g in range(2):
             wt = lax.dot_general(
                 coef_ref[g], err, (((1,), (1,)), ((), ())),
                 precision=lax.Precision.HIGHEST, preferred_element_type=jnp.float32,
-            ) * (W / PIX / ALPHA)
+            ) * (W * Q / PIX)
             for t in range(16):
                 weight_ref[g, t] = jnp.broadcast_to(wt[:, t:t + 1], (8, LANES))
 
@@ -330,41 +316,66 @@
                 ] + [w * unit_ref[step, i, half, 1 + h, r] for h in range(3)]
                 acc = [b if a is None else a + b for a, b in zip(acc, terms)]
         for k in range(6):
-            acc_ref[part, k, r] = acc[k]
-
-    @pl.when(part == 1)
+            acc_ref[step, k, r] = acc[k]
+
+    @pl.when(step == 3)
     def _():
         R = range(8)
 
-        def variance(h):
+        def variance(g, h):
             return [
                 -(sup_ref[g, 3 + h, r] * sup_ref[g, 3 + h, r])
-                * (acc_ref[0, 3 + h, r] + acc_ref[1, 3 + h, r])
+                * (acc_ref[2 * g, 3 + h, r] + acc_ref[2 * g + 1, 3 + h, r])
                 for r in R
             ]
 
-        gn = variance(2)
+        G = range(2)
+        gn = [variance(g, 2) for g in G]
         for h in (1, 0):
-            back = box(gn, masks)
-            own = variance(h)
-            gn = [own[r] + ALPHA * back[r] * sup_ref[g, 6 + h, r] for r in R]
-        back = box(gn, masks)
+            back = [box(gn[g], masks) for g in G]
+            own = [variance(g, h) for g in G]
+            gn = [[own[g][r] + ALPHA * back[g][r] * sup_ref[g, 6 + h, r] for r in R] for g in G]
+        back = [box(gn[g], masks) for g in G]
         for ch in range(CH):
-            v = [
-                acc_ref[0, ch, r] + acc_ref[1, ch, r]
-                + (2.0 * ALPHA / CH) * sup_ref[g, ch, r] * back[r]
-                for r in R
-            ]
-            nat = deinterleave(v, masks)
-            for m in range(8):
-                for b in range(2):
-                    grad_ref[pl.ds(m * 48 + ch * 4 + 2 * g + b, 4, stride=12), :] = nat[m][4 * b:4 * b + 4]
+            for g in G:
+                v = [
+                    acc_ref[2 * g, ch, r] + acc_ref[2 * g + 1, ch, r]
+                    + (2.0 * ALPHA / CH) * sup_ref[g, ch, r] * back[g][r]
+                    for r in R
+                ]
+                nat = exchange_blocks(v, masks)
+                for m in range(8):
+                    for b in range(2):
+                        grad_ref[pl.ds(m * 48 + ch * 4 + 2 * g + b, 4, stride=12), :] = nat[m][4 * b:4 * b + 4]
 
 
 VMEM = pltpu.MemorySpace.VMEM
 SMEM = pltpu.MemorySpace.SMEM
 FULL = pl.BlockSpec(memory_space=VMEM)
 PARAMS = pltpu.CompilerParams(vmem_limit_bytes=24 * 2**20)
+
+
+def fold_kernel(parts_ref, out_ref):
+    vs = [parts_ref[k * 24:k * 24 + 24, :] for k in range(parts_ref.shape[0] // 24)]
+    while len(vs) > 1:
+        vs = [a + b for a, b in zip(vs[::2], vs[1::2])]
+    half = vs[0].shape[0] // 2
+    piece = vs[0][:half] + vs[0][half:]
+    twice = jnp.concatenate([piece, piece], axis=0)
+    natural = jnp.broadcast_to(lane_masks()[2][0:1], twice.shape)
+    twice = jnp.take_along_axis(twice, natural, axis=1)
+    for k in range(out_ref.shape[0] // 24):
+        out_ref[k * 24:k * 24 + 24, :] = twice
+
+
+def fold_call(parts):
+    return pl.pallas_call(
+        fold_kernel,
+        in_specs=[FULL], out_specs=FULL,
+        out_shape=jax.ShapeDtypeStruct(parts.shape, jnp.float32),
+        compiler_params=PARAMS,
+        name="fold",
+    )(parts)
 
 
 def slot_call(slot):
@@ -401,6 +412,8 @@
         blocks = [jnp.where(o == slot, v, a) for o, a in zip(owners, blocks)]
     piece = [v[ch:ch + 1] for ch in range(CH) for v in blocks]
     twice = jnp.concatenate(piece + piece, axis=0)
+    tiled = jnp.broadcast_to(lane_masks()[1][0:1], twice.shape)
+    twice = jnp.take_along_axis(twice, tiled, axis=1)
     for k in range(out_ref.shape[0] // twice.shape[0]):
         out_ref[k * twice.shape[0]:(k + 1) * twice.shape[0], :] = twice
 
@@ -458,12 +471,9 @@
             FULL,
             FULL,
         ],
-        out_specs=[FULL, FULL],
-        out_shape=[
-            jax.ShapeDtypeStruct((8, LANES), f32),
-            jax.ShapeDtypeStruct((384, LANES), f32),
-        ],
-        scratch_shapes=[pltpu.VMEM((2, 16, 8, LANES), f32), pltpu.VMEM((2, 6, 8, 8, LANES), f32)],
+        out_specs=FULL,
+        out_shape=jax.ShapeDtypeStruct((384, LANES), f32),
+        scratch_shapes=[pltpu.VMEM((2, 16, 8, LANES), f32), pltpu.VMEM((4, 6, 8, 8, LANES), f32)],
         compiler_params=PARAMS,
         name="weigh",
     )(core, parts, unit, own, other, sup, coef)
@@ -496,19 +506,20 @@
     parts = lax.all_to_all(
         parts, ("tgt", "sup"), 0, 0, axis_index_groups=sets, tiled=True
     )
-    pred, grad = weigh_call(classes, core, parts, unit, own, other, sup, coef)
+    grad = weigh_call(classes, core, parts, unit, own, other, sup, coef)
     grad = lax.all_to_all(
         grad.reshape(piece_shape), "tgt", 0, 0, axis_index_groups=planes, tiled=True
     )
-    piece = jnp.sum(grad, axis=0, keepdims=True)
+    full = fold_call(grad.reshape(half_n * blocks * CH, LANES)).reshape(piece_shape)
     full = lax.all_to_all(
-        jnp.broadcast_to(piece, piece_shape), "tgt", 0, 0, axis_index_groups=planes, tiled=True
+        full, "tgt", 0, 0, axis_index_groups=planes, tiled=True
     )
     theirs = lax.ppermute(full, "tgt", partner)
     even = jnp.where(core[0] == 0, full, theirs)
     odd = jnp.where(core[0] == 0, theirs, full)
     both = jnp.stack([even, odd]).reshape(2, 8, 4, CH, blocks, LANES)
     out = both.transpose(4, 2, 0, 3, 1, 5).reshape(blocks, 8, CH, PIX)
+    pred = jnp.sum(lax.dynamic_slice_in_dim(parts, core[0] * 8, 8, 1), axis=0)
     return pred[:, :classes], out
 
 

time: 115 us -> 113 us (0.983)
  transfers between devices with their start and end apart: 4 -> 4, of which waited for: 4 -> 4; matrix products, arithmetic and copies ran while one was open for 1% -> 2% of each run, Pallas kernels for 1% -> 1%
where the time goes in v4:
time: 113 us
  blocking collectives  45.1 us (40%)
  starting transfers between devices  28.2 us (25%)
  waiting for transfers between devices  18.2 us (16%)
  Pallas kernels  15 us (13%)
  local copies, waits for them, and re-layouts  4.24 us (4%)
  other arithmetic  1.37 us (1%)
    all_to_all x1, starting transfers between devices, local(): got = lax.all_to_all(slot, 'tgt', 0, 0, tiled=True)  17.6 us
    all_to_all x1, blocking collectives, local(): lax.all_to_all(full, 'tgt', 0, 0, axis_index_groups=planes, tiled=True)  16.8 us
    all_to_all x1, blocking collectives, local(): lax.all_to_all(grad.reshape(piece_shape), 'tgt', 0, 0, axis_index_groups=...  15.3 us
    all_to_all x1, blocking collectives, local(): lax.all_to_all(parts, ('tgt', 'sup'), 0, 0, axis_index_groups=sets, tiled...  13 us
    pallas_call x1, Pallas kernels, main_call(): pl.pallas_call(main_kernel, grid=(4,), in_specs=[pl.BlockSpec(memory_spac...  10.3 us
    all_to_all x1, waiting for transfers between devices, local(): got = lax.all_to_all(slot, 'tgt', 0, 0, tiled=True)  9.4 us
    all_to_all x1, waiting for transfers between devices, local(): lax.all_to_all(pick_call(owner, got, half_n).reshape(piece_shape), 'tgt',...  8.1 us
    ppermute x1, starting transfers between devices, local(): theirs = lax.ppermute(full, 'tgt', partner)  4.42 us
  transfers between devices with their start and end apart: 4, of which 4 were waited for; matrix products, arithmetic and copies ran while one was open for 2% of the time, Pallas kernels for 1%

profile of v4, /device:TPU:1, one launch (start us, length us, event | category | flops | bytes accessed | tf_op | source)
XLA Modules:
  0.0 112.9 jit_solution(1119946356876567172)
XLA Ops:
  0.6 0.0 copy-start
  0.6 0.9 copy-done
  1.5 0.7 slot.1
  2.2 17.6 %all-to-all-start = ((f32[64,4,128]{2,1,0:T(4,128)}), f32[64,4,128]{2,1,0:T(4,128)S(1)}, u32[]{:S(2)}, u32[]{:S(2)}) async-start(f32[64,4,128]{2,1,0:T(4,128)} %bitcast.3), calls=%async_computation | async-start | bytes 262144 | tf_op jit(solution)/shard_map/all_to_all | solution.py:493
  19.8 1.0 copy.7.images_ref
  20.8 0.0 copy-start.1
  20.8 0.7 copy-done.1
  21.5 0.0 copy-start.2
  21.5 0.7 copy-done.2
  22.2 1.4 %targets.1 = (f32[6,8,8,128]{3,2,1,0:T(8,128)S(1)}, f32[2,8,128]{2,1,0:T(8,128)S(1)}, s32[4,128]{1,0:T(4,128)S(1)}) custom-call(s32[1]{0:T(128)} %bitcast.core_ref, s32[4]{0:T(128)S(1)} %copy-done.2, f32[8,3,1024]{2,1,0:T(4,128)S(1)} %copy.7.images_ref, f32[4,8,100]{2,1,0:T(8,128)S(1)} %copy-done.1), custom_call_target="tpu_custom_call" | custom-call | tf_op jit(solution)/shard_map/targets/pallas_call | solution.py:393
  23.5 9.4 %all-to-all-done.got_ref = f32[64,4,128]{2,1,0:T(4,128)S(1)} async-done(((f32[64,4,128]{2,1,0:T(4,128)}), f32[64,4,128]{2,1,0:T(4,128)S(1)}, u32[]{:S(2)}, u32[]{:S(2)}) %all-to-all-start) | async-done | bytes 131104 | tf_op jit(solution)/shard_map/all_to_all | solution.py:493
  32.9 0.8 pick.1
  33.8 3.9 %all-to-all-start.1 = ((f32[32,3,4,128]{3,2,1,0:T(4,128)}), f32[32,3,4,128]{3,2,1,0:T(4,128)S(1)}, u32[]{:S(2)}, u32[]{:S(2)}) async-start(f32[32,3,4,128]{3,2,1,0:T(4,128)} %bitcast.4), calls=%async_computation.1 | async-start | bytes 393216 | tf_op jit(solution)/shard_map/all_to_all | solution.py:499
  37.7 2.3 %collective-permute-start = (f32[6,8,8,128]{3,2,1,0:T(8,128)S(1)}, f32[6,8,8,128]{3,2,1,0:T(8,128)S(1)}, u32[]{:S(2)}, u32[]{:S(2)}) collective-permute-start(f32[6,8,8,128]{3,2,1,0:T(8,128)S(1)} %get-tuple-element.13.own_ref), channel_id=1, source_target_pairs={{0,8},{8,0},{16,24},{24,16},{32,40},{40,32},{48,56},{56,48},{64,72... | collective-permute-start | bytes 589832 | tf_op jit(solution)/shard_map/ppermute | solution.py:496
  40.0 0.7 fusion
  40.7 0.1 copy.8.label_ref
  40.7 0.3 collective-permute-done.other_ref
  41.0 8.1 %all-to-all-done.1 = f32[32,3,4,128]{3,2,1,0:T(4,128)S(1)} async-done(((f32[32,3,4,128]{3,2,1,0:T(4,128)}), f32[32,3,4,128]{3,2,1,0:T(4,128)S(1)}, u32[]{:S(2)}, u32[]{:S(2)}) %all-to-all-start.1) | async-done | bytes 196640 | tf_op jit(solution)/shard_map/all_to_all | solution.py:499
  49.1 10.3 %pairs.1 = (f32[16,16,128]{2,1,0:T(8,128)S(1)}, f32[4,4,2,4,8,8,128]{6,5,4,3,2,1,0:T(8,128)S(1)}, f32[2,8,8,8,128]{4,3,2,1,0:T(8,128)S(1)}) custom-call(s32[1]{0:T(128)} %bitcast.core_ref, f32[6,8,8,128]{3,2,1,0:T(8,128)S(1)} %get-tuple-element.13.own_ref, f32[6,8,8,128]{3,2,1,0:T(8,128)S(1)} %collective-permute-done.other_ref, f32[384,128]{1,0:T(8,128)S(1)} %bitcast.24, ...), custom_call_target="tpu_custom_call" | custom-call | tf_op jit(solution)/shard_map/pairs/pallas_call | solution.py:437
  59.5 13.0 %all_to_all.25.parts_ref = f32[16,16,128]{2,1,0:T(8,128)S(1)} all-to-all(f32[16,16,128]{2,1,0:T(8,128)S(1)} %get-tuple-element.17), channel_id=1, replica_groups={{0,1,2,3,4,5,6,7,8,9,10,11,12,13,14,15},{16,17,18,19,20,21,22,23,24,25,..., dimensions={0} | all-to-all | bytes 262144 | tf_op jit(solution)/shard_map/all_to_all | solution.py:506
  72.5 1.7 %weigh.1 = f32[384,128]{1,0:T(8,128)S(1)} custom-call(s32[1]{0:T(128)} %bitcast.core_ref, f32[16,16,128]{2,1,0:T(8,128)S(1)} %all_to_all.25.parts_ref, f32[4,4,2,4,8,8,128]{6,5,4,3,2,1,0:T(8,128)S(1)} %get-tuple-element.18.unit_ref, f32[6,8,8,128]{3,2,1,0:T(8,128)S(1)} %get-tuple-element.13.own_ref, f32[6,8,8,128]{3,2,1,0:T(8,128)S(1)} %collective-permute-done.other_ref, ...), custom_call_target="tpu_custom_call" | custom-call | tf_op jit(solution)/shard_map/weigh/pallas_call | solution.py:463
  74.1 15.3 %all_to_all.26 = f32[32,3,4,128]{3,2,1,0:T(4,128)S(1)} all-to-all(f32[32,3,4,128]{3,2,1,0:T(4,128)S(1)} %bitcast.21), channel_id=1, replica_groups={{0,16,32,48,64,80,96,112,128,144,160,176,192,208,224,240,256,272,288,30..., dimensions={0} | all-to-all | bytes 393216 | tf_op jit(solution)/shard_map/all_to_all | solution.py:510
  89.4 0.1 fold.1
  89.5 16.8 %all_to_all.27 = f32[32,3,4,128]{3,2,1,0:T(4,128)S(1)} all-to-all(f32[32,3,4,128]{3,2,1,0:T(4,128)S(1)} %bitcast.23), channel_id=1, replica_groups={{0,16,32,48,64,80,96,112,128,144,160,176,192,208,224,240,256,272,288,30..., dimensions={0} | all-to-all | bytes 393216 | tf_op jit(solution)/shard_map/all_to_all | solution.py:514
  106.4 4.4 %collective-permute-start.1 = (f32[32,3,4,128]{3,2,1,0:T(4,128)S(1)}, f32[32,3,4,128]{3,2,1,0:T(4,128)S(1)}, u32[]{:S(2)}, u32[]{:S(2)}) collective-permute-start(f32[32,3,4,128]{3,2,1,0:T(4,128)S(1)} %all_to_all.27), channel_id=1, source_target_pairs={{0,8},{8,0},{16,24},{24,16},{32,40},{40,32},{48,56},{56,48},{64,72... | collective-permute-start | bytes 589832 | tf_op jit(solution)/shard_map/ppermute | solution.py:517
  110.8 0.6 dynamic-slice_reduce_fusion
  111.4 0.4 collective-permute-done.1
  111.8 0.1 broadcast_select_fusion.1
  111.9 0.1 copy.10
  112.0 0.1 copy.9
  112.1 0.8 reshape.36
  (1 shorter events, 0.0 us)
Async XLA Ops:
  0.6 0.9 copy-start
  2.2 30.8 %all-to-all-start = ((f32[64,4,128]{2,1,0:T(4,128)}), f32[64,4,128]{2,1,0:T(4,128)S(1)}, u32[]{:S(2)}, u32[]{:S(2)}) async-start(f32[64,4,128]{2,1,0:T(4,128)} %bitcast.3), calls=%async_computation | async-start | bytes 262144 | tf_op jit(solution)/shard_map/all_to_all | solution.py:493
  20.8 0.7 copy-start.1
  21.5 0.7 copy-start.2
  33.8 15.4 %all-to-all-start.1 = ((f32[32,3,4,128]{3,2,1,0:T(4,128)}), f32[32,3,4,128]{3,2,1,0:T(4,128)S(1)}, u32[]{:S(2)}, u32[]{:S(2)}) async-start(f32[32,3,4,128]{3,2,1,0:T(4,128)} %bitcast.4), calls=%async_computation.1 | async-start | bytes 393216 | tf_op jit(solution)/shard_map/all_to_all | solution.py:499
  37.7 3.4 %collective-permute-start = (f32[6,8,8,128]{3,2,1,0:T(8,128)S(1)}, f32[6,8,8,128]{3,2,1,0:T(8,128)S(1)}, u32[]{:S(2)}, u32[]{:S(2)}) collective-permute-start(f32[6,8,8,128]{3,2,1,0:T(8,128)S(1)} %get-tuple-element.13.own_ref), channel_id=1, source_target_pairs={{0,8},{8,0},{16,24},{24,16},{32,40},{40,32},{48,56},{56,48},{64,72... | collective-permute-start | bytes 589832 | tf_op jit(solution)/shard_map/ppermute | solution.py:496
  106.4 5.5 %collective-permute-start.1 = (f32[32,3,4,128]{3,2,1,0:T(4,128)S(1)}, f32[32,3,4,128]{3,2,1,0:T(4,128)S(1)}, u32[]{:S(2)}, u32[]{:S(2)}) collective-permute-start(f32[32,3,4,128]{3,2,1,0:T(4,128)S(1)} %all_to_all.27), channel_id=1, source_target_pairs={{0,8},{8,0},{16,24},{24,16},{32,40},{40,32},{48,56},{56,48},{64,72... | collective-permute-start | bytes 589832 | tf_op jit(solution)/shard_map/ppermute | solution.py:517

commit v5 on v4

--- a/solution.py
+++ b/solution.py
@@ -104,9 +104,7 @@
 def slot_kernel(slot_ref, out_ref):
     for ch in range(CH):
         for m in range(8):
-            out_ref[pl.ds(m * 32 + ch, 8, stride=4), :] = slot_ref[ch, :, m * LANES:(m + 1) * LANES]
-    for m in range(8):
-        out_ref[pl.ds(m * 32 + CH, 8, stride=4), :] = jnp.zeros((8, LANES), jnp.float32)
+            out_ref[pl.ds(m * 24 + ch, 8, stride=3), :] = slot_ref[ch, :, m * LANES:(m + 1) * LANES]
 
 
 def target_kernel(core_ref, owner_ref, images_ref, coef_ref, out_ref, rows_ref, lanes_ref):
@@ -382,7 +380,7 @@
     return pl.pallas_call(
         slot_kernel,
         in_specs=[FULL], out_specs=FULL,
-        out_shape=jax.ShapeDtypeStruct((256, LANES), jnp.float32),
+        out_shape=jax.ShapeDtypeStruct((192, LANES), jnp.float32),
         compiler_params=PARAMS,
         name="slot",
     )(slot)
@@ -405,12 +403,21 @@
 
 
 def pick_kernel(owner_ref, got_ref, out_ref):
-    blocks = [jnp.zeros(got_ref.shape[1:], jnp.float32)] * owner_ref.shape[0]
-    owners = [jnp.broadcast_to(owner_ref[b:b + 1, :], got_ref.shape[1:]) for b in range(len(blocks))]
-    for slot in range(got_ref.shape[0]):
-        v = got_ref[slot]
-        blocks = [jnp.where(o == slot, v, a) for o, a in zip(owners, blocks)]
-    piece = [v[ch:ch + 1] for ch in range(CH) for v in blocks]
+    count = owner_ref.shape[0]
+    rows = 8 * CH
+    place = lax.broadcasted_iota(jnp.int32, (rows, LANES), 0) // CH
+    blocks = [jnp.zeros((rows, LANES), jnp.float32)] * count
+    owners = [jnp.broadcast_to(owner_ref[b:b + 1, :], (rows, LANES)) - place for b in range(count)]
+    for k in range(got_ref.shape[0] // rows):
+        v = got_ref[k * rows:(k + 1) * rows, :]
+        blocks = [jnp.where(o == 8 * k, v, a) for o, a in zip(owners, blocks)]
+    sums = []
+    for a in blocks:
+        parts = [a[CH * k:CH * (k + 1)] for k in range(8)]
+        while len(parts) > 1:
+            parts = [x + y for x, y in zip(parts[::2], parts[1::2])]
+        sums.append(parts[0])
+    piece = [v[ch:ch + 1] for ch in range(CH) for v in sums]
     twice = jnp.concatenate(piece + piece, axis=0)
     tiled = jnp.broadcast_to(lane_masks()[1][0:1], twice.shape)
     twice = jnp.take_along_axis(twice, tiled, axis=1)
@@ -489,7 +496,7 @@
     sets = [
         [t * sup_n + s for t in (2 * k, 2 * k + 1) for s in range(sup_n)] for k in range(tgt_n // 2)
     ]
-    slot = slot_call(support_slots[0].transpose(1, 0, 2)).reshape(tgt_n, 4, LANES)
+    slot = slot_call(support_slots[0].transpose(1, 0, 2)).reshape(tgt_n, 1, CH * LANES)
     got = lax.all_to_all(slot, "tgt", 0, 0, tiled=True)
     own, coef, owner = target_call(core, block_owner, targets, dual_coeffs)
     got, own, owner = lax.optimization_barrier((got, own, owner))
@@ -497,7 +504,7 @@
     half_n = tgt_n // 2
     piece_shape = (half_n, CH, blocks, LANES)
     rows = lax.all_to_all(
-        pick_call(owner, got, half_n).reshape(piece_shape), "tgt", 0, 0,
+        pick_call(owner, got.reshape(tgt_n * CH, LANES), half_n).reshape(piece_shape), "tgt", 0, 0,
         axis_index_groups=planes, tiled=True,
     ).reshape(half_n * blocks * CH, LANES)
     first = lax.axis_index("sup") == 0

time: 113 us -> 113 us (level)
  no operation moved by 1% of the time
where the time goes in v5:
time: 113 us; the launch traced here: 112 us
  blocking collectives  44.8 us (40%)
  starting transfers between devices  28.2 us (25%)
  waiting for transfers between devices  17.9 us (16%)
  Pallas kernels  14.9 us (13%)
  local copies, waits for them, and re-layouts  4.24 us (4%)
  other arithmetic  1.37 us (1%)
    all_to_all x1, starting transfers between devices, local(): got = lax.all_to_all(slot, 'tgt', 0, 0, tiled=True)  17.6 us
    all_to_all x1, blocking collectives, local(): lax.all_to_all(full, 'tgt', 0, 0, axis_index_groups=planes, tiled=True)  16.8 us
    all_to_all x1, blocking collectives, local(): lax.all_to_all(grad.reshape(piece_shape), 'tgt', 0, 0, axis_index_groups=...  15.3 us
    all_to_all x1, blocking collectives, local(): lax.all_to_all(parts, ('tgt', 'sup'), 0, 0, axis_index_groups=sets, tiled...  12.7 us
    pallas_call x1, Pallas kernels, main_call(): pl.pallas_call(main_kernel, grid=(4,), in_specs=[pl.BlockSpec(memory_spac...  10.3 us
    all_to_all x1, waiting for transfers between devices, local(): got = lax.all_to_all(slot, 'tgt', 0, 0, tiled=True)  8.95 us
    all_to_all x1, waiting for transfers between devices, local(): lax.all_to_all(pick_call(owner, got.reshape(tgt_n * CH, LANES), half_n).r...  8.25 us
    ppermute x1, starting transfers between devices, local(): theirs = lax.ppermute(full, 'tgt', partner)  4.42 us
  transfers between devices with their start and end apart: 4, of which 4 were waited for; matrix products, arithmetic and copies ran while one was open for 2% of the time, Pallas kernels for 1%

profile of v5, /device:TPU:1, one launch (start us, length us, event | category | flops | bytes accessed | tf_op | source)
XLA Modules:
  0.0 112.2 jit_solution(8398459045281470238)
XLA Ops:
  0.6 0.0 copy-start
  0.6 0.9 copy-done
  1.5 0.6 slot.1
  2.2 17.6 %all-to-all-start = ((f32[64,1,384]{2,1,0:T(1,128)}), f32[64,1,384]{2,1,0:T(1,128)S(1)}, u32[]{:S(2)}, u32[]{:S(2)}) async-start(f32[64,1,384]{2,1,0:T(1,128)} %bitcast.3), calls=%async_computation | async-start | bytes 196608 | tf_op jit(solution)/shard_map/all_to_all | solution.py:500
  19.8 1.0 copy.12.images_ref
  20.8 0.0 copy-start.1
  20.8 0.7 copy-done.1
  21.5 0.0 copy-start.2
  21.5 0.7 copy-done.2
  22.2 1.4 %targets.1 = (f32[6,8,8,128]{3,2,1,0:T(8,128)S(1)}, f32[2,8,128]{2,1,0:T(8,128)S(1)}, s32[4,128]{1,0:T(4,128)S(1)}) custom-call(s32[1]{0:T(128)} %bitcast.core_ref, s32[4]{0:T(128)S(1)} %copy-done.2, f32[8,3,1024]{2,1,0:T(4,128)S(1)} %copy.12.images_ref, f32[4,8,100]{2,1,0:T(8,128)S(1)} %copy-done.1), custom_call_target="tpu_custom_call" | custom-call | tf_op jit(solution)/shard_map/targets/pallas_call | solution.py:391
  23.5 9.0 %all-to-all-done = f32[64,1,384]{2,1,0:T(1,128)S(1)} async-done(((f32[64,1,384]{2,1,0:T(1,128)}), f32[64,1,384]{2,1,0:T(1,128)S(1)}, u32[]{:S(2)}, u32[]{:S(2)}) %all-to-all-start) | async-done | bytes 98336 | tf_op jit(solution)/shard_map/all_to_all | solution.py:500
  32.5 0.8 pick.1
  33.3 3.9 %all-to-all-start.1 = ((f32[32,3,4,128]{3,2,1,0:T(4,128)}), f32[32,3,4,128]{3,2,1,0:T(4,128)S(1)}, u32[]{:S(2)}, u32[]{:S(2)}) async-start(f32[32,3,4,128]{3,2,1,0:T(4,128)} %bitcast.5), calls=%async_computation.1 | async-start | bytes 393216 | tf_op jit(solution)/shard_map/all_to_all | solution.py:506
  37.2 2.3 %collective-permute-start = (f32[6,8,8,128]{3,2,1,0:T(8,128)S(1)}, f32[6,8,8,128]{3,2,1,0:T(8,128)S(1)}, u32[]{:S(2)}, u32[]{:S(2)}) collective-permute-start(f32[6,8,8,128]{3,2,1,0:T(8,128)S(1)} %get-tuple-element.13.own_ref), channel_id=1, source_target_pairs={{0,8},{8,0},{16,24},{24,16},{32,40},{40,32},{48,56},{56,48},{64,72... | collective-permute-start | bytes 589832 | tf_op jit(solution)/shard_map/ppermute | solution.py:503
  39.5 0.7 fusion
  40.1 0.1 copy.13.label_ref
  40.2 0.3 collective-permute-done.other_ref
  40.5 8.2 %all-to-all-done.1 = f32[32,3,4,128]{3,2,1,0:T(4,128)S(1)} async-done(((f32[32,3,4,128]{3,2,1,0:T(4,128)}), f32[32,3,4,128]{3,2,1,0:T(4,128)S(1)}, u32[]{:S(2)}, u32[]{:S(2)}) %all-to-all-start.1) | async-done | bytes 196640 | tf_op jit(solution)/shard_map/all_to_all | solution.py:506
  48.8 10.3 %pairs.1 = (f32[16,16,128]{2,1,0:T(8,128)S(1)}, f32[4,4,2,4,8,8,128]{6,5,4,3,2,1,0:T(8,128)S(1)}, f32[2,8,8,8,128]{4,3,2,1,0:T(8,128)S(1)}) custom-call(s32[1]{0:T(128)} %bitcast.core_ref, f32[6,8,8,128]{3,2,1,0:T(8,128)S(1)} %get-tuple-element.13.own_ref, f32[6,8,8,128]{3,2,1,0:T(8,128)S(1)} %collective-permute-done.other_ref, f32[384,128]{1,0:T(8,128)S(1)} %bitcast.25, ...), custom_call_target="tpu_custom_call" | custom-call | tf_op jit(solution)/shard_map/pairs/pallas_call | solution.py:444
  59.1 12.7 %all_to_all.25.parts_ref = f32[16,16,128]{2,1,0:T(8,128)S(1)} all-to-all(f32[16,16,128]{2,1,0:T(8,128)S(1)} %get-tuple-element.17), channel_id=1, replica_groups={{0,1,2,3,4,5,6,7,8,9,10,11,12,13,14,15},{16,17,18,19,20,21,22,23,24,25,..., dimensions={0} | all-to-all | bytes 262144 | tf_op jit(solution)/shard_map/all_to_all | solution.py:513
  71.8 1.7 %weigh.1 = f32[384,128]{1,0:T(8,128)S(1)} custom-call(s32[1]{0:T(128)} %bitcast.core_ref, f32[16,16,128]{2,1,0:T(8,128)S(1)} %all_to_all.25.parts_ref, f32[4,4,2,4,8,8,128]{6,5,4,3,2,1,0:T(8,128)S(1)} %get-tuple-element.18.unit_ref, f32[6,8,8,128]{3,2,1,0:T(8,128)S(1)} %get-tuple-element.13.own_ref, f32[6,8,8,128]{3,2,1,0:T(8,128)S(1)} %collective-permute-done.other_ref, ...), custom_call_target="tpu_custom_call" | custom-call | tf_op jit(solution)/shard_map/weigh/pallas_call | solution.py:470
  73.5 15.3 %all_to_all.26 = f32[32,3,4,128]{3,2,1,0:T(4,128)S(1)} all-to-all(f32[32,3,4,128]{3,2,1,0:T(4,128)S(1)} %bitcast.22), channel_id=1, replica_groups={{0,16,32,48,64,80,96,112,128,144,160,176,192,208,224,240,256,272,288,30..., dimensions={0} | all-to-all | bytes 393216 | tf_op jit(solution)/shard_map/all_to_all | solution.py:517
  88.7 0.1 fold.1
  88.9 16.8 %all_to_all.27 = f32[32,3,4,128]{3,2,1,0:T(4,128)S(1)} all-to-all(f32[32,3,4,128]{3,2,1,0:T(4,128)S(1)} %bitcast.24), channel_id=1, replica_groups={{0,16,32,48,64,80,96,112,128,144,160,176,192,208,224,240,256,272,288,30..., dimensions={0} | all-to-all | bytes 393216 | tf_op jit(solution)/shard_map/all_to_all | solution.py:521
  105.7 4.4 %collective-permute-start.1 = (f32[32,3,4,128]{3,2,1,0:T(4,128)S(1)}, f32[32,3,4,128]{3,2,1,0:T(4,128)S(1)}, u32[]{:S(2)}, u32[]{:S(2)}) collective-permute-start(f32[32,3,4,128]{3,2,1,0:T(4,128)S(1)} %all_to_all.27), channel_id=1, source_target_pairs={{0,8},{8,0},{16,24},{24,16},{32,40},{40,32},{48,56},{56,48},{64,72... | collective-permute-start | bytes 589832 | tf_op jit(solution)/shard_map/ppermute | solution.py:524
  110.1 0.6 dynamic-slice_reduce_fusion
  110.7 0.4 collective-permute-done.1
  111.2 0.1 broadcast_select_fusion.1
  111.2 0.1 copy.14
  111.3 0.1 copy.15
  111.4 0.8 reshape.40
  (1 shorter events, 0.0 us)
Async XLA Ops:
  0.6 0.9 copy-start
  2.2 30.3 %all-to-all-start = ((f32[64,1,384]{2,1,0:T(1,128)}), f32[64,1,384]{2,1,0:T(1,128)S(1)}, u32[]{:S(2)}, u32[]{:S(2)}) async-start(f32[64,1,384]{2,1,0:T(1,128)} %bitcast.3), calls=%async_computation | async-start | bytes 196608 | tf_op jit(solution)/shard_map/all_to_all | solution.py:500
  20.8 0.7 copy-start.1
  21.5 0.7 copy-start.2
  33.3 15.5 %all-to-all-start.1 = ((f32[32,3,4,128]{3,2,1,0:T(4,128)}), f32[32,3,4,128]{3,2,1,0:T(4,128)S(1)}, u32[]{:S(2)}, u32[]{:S(2)}) async-start(f32[32,3,4,128]{3,2,1,0:T(4,128)} %bitcast.5), calls=%async_computation.1 | async-start | bytes 393216 | tf_op jit(solution)/shard_map/all_to_all | solution.py:506
  37.2 3.4 %collective-permute-start = (f32[6,8,8,128]{3,2,1,0:T(8,128)S(1)}, f32[6,8,8,128]{3,2,1,0:T(8,128)S(1)}, u32[]{:S(2)}, u32[]{:S(2)}) collective-permute-start(f32[6,8,8,128]{3,2,1,0:T(8,128)S(1)} %get-tuple-element.13.own_ref), channel_id=1, source_target_pairs={{0,8},{8,0},{16,24},{24,16},{32,40},{40,32},{48,56},{56,48},{64,72... | collective-permute-start | bytes 589832 | tf_op jit(solution)/shard_map/ppermute | solution.py:503
  105.7 5.5 %collective-permute-start.1 = (f32[32,3,4,128]{3,2,1,0:T(4,128)S(1)}, f32[32,3,4,128]{3,2,1,0:T(4,128)S(1)}, u32[]{:S(2)}, u32[]{:S(2)}) collective-permute-start(f32[32,3,4,128]{3,2,1,0:T(4,128)S(1)} %all_to_all.27), channel_id=1, source_target_pairs={{0,8},{8,0},{16,24},{24,16},{32,40},{40,32},{48,56},{56,48},{64,72... | collective-permute-start | bytes 589832 | tf_op jit(solution)/shard_map/ppermute | solution.py:524

commit v6 on v5

--- a/solution.py
+++ b/solution.py
@@ -379,9 +379,10 @@
 def slot_call(slot):
     return pl.pallas_call(
         slot_kernel,
-        in_specs=[FULL], out_specs=FULL,
+        grid=(1,),
+        in_specs=[pl.BlockSpec(slot.shape, lambda i: (0, 0, 0))], out_specs=FULL,
         out_shape=jax.ShapeDtypeStruct((192, LANES), jnp.float32),
-        compiler_params=PARAMS,
+        compiler_params=pltpu.CompilerParams(vmem_limit_bytes=63 * 2**20),
         name="slot",
     )(slot)
 

time: 113 us -> 113 us (level)
    unnamed x7 -> x5, local copies, waits for them, and re-layouts: 3.22 us -> 2.33 us
where the time goes in v6:
time: 113 us; the launch traced here: 112 us
  blocking collectives  44.8 us (40%)
  starting transfers between devices  28.2 us (25%)
  waiting for transfers between devices  17.9 us (16%)
  Pallas kernels  15.8 us (14%)
  local copies, waits for them, and re-layouts  3.36 us (3%)
  other arithmetic  1.37 us (1%)
    all_to_all x1, starting transfers between devices, local(): got = lax.all_to_all(slot, 'tgt', 0, 0, tiled=True)  17.6 us
    all_to_all x1, blocking collectives, local(): lax.all_to_all(full, 'tgt', 0, 0, axis_index_groups=planes, tiled=True)  16.8 us
    all_to_all x1, blocking collectives, local(): lax.all_to_all(grad.reshape(piece_shape), 'tgt', 0, 0, axis_index_groups=...  15.3 us
    all_to_all x1, blocking collectives, local(): lax.all_to_all(parts, ('tgt', 'sup'), 0, 0, axis_index_groups=sets, tiled...  12.7 us
    pallas_call x1, Pallas kernels, main_call(): pl.pallas_call(main_kernel, grid=(4,), in_specs=[pl.BlockSpec(memory_spac...  10.4 us
    all_to_all x1, waiting for transfers between devices, local(): got = lax.all_to_all(slot, 'tgt', 0, 0, tiled=True)  8.95 us
    all_to_all x1, waiting for transfers between devices, local(): lax.all_to_all(pick_call(owner, got.reshape(tgt_n * CH, LANES), half_n).r...  8.25 us
    ppermute x1, starting transfers between devices, local(): theirs = lax.ppermute(full, 'tgt', partner)  4.42 us
  transfers between devices with their start and end apart: 4, of which 4 were waited for; matrix products, arithmetic and copies ran while one was open for 2% of the time, Pallas kernels for 1%

profile of v6, /device:TPU:1, one launch (start us, length us, event | category | flops | bytes accessed | tf_op | source)
XLA Modules:
  0.0 112.3 jit_solution(13701802272815436759)
XLA Ops:
  0.6 1.5 %slot.1 = f32[192,128]{1,0:T(8,128)} custom-call(f32[3,8,1024]{2,1,0:T(8,128)} %bitcast.30), custom_call_target="tpu_custom_call" | custom-call | tf_op jit(solution)/shard_map/slot/pallas_call | solution.py:380
  2.2 17.6 %all-to-all-start = ((f32[64,1,384]{2,1,0:T(1,128)}), f32[64,1,384]{2,1,0:T(1,128)S(1)}, u32[]{:S(2)}, u32[]{:S(2)}) async-start(f32[64,1,384]{2,1,0:T(1,128)} %bitcast.29), calls=%async_computation | async-start | bytes 196608 | tf_op jit(solution)/shard_map/all_to_all | solution.py:501
  19.8 1.0 copy.12.images_ref
  20.8 0.0 copy-start
  20.8 0.7 copy-done
  21.5 0.0 copy-start.1
  21.5 0.7 copy-done.1
  22.2 1.4 %targets.1 = (f32[6,8,8,128]{3,2,1,0:T(8,128)S(1)}, f32[2,8,128]{2,1,0:T(8,128)S(1)}, s32[4,128]{1,0:T(4,128)S(1)}) custom-call(s32[1]{0:T(128)} %bitcast.core_ref, s32[4]{0:T(128)S(1)} %copy-done.1, f32[8,3,1024]{2,1,0:T(4,128)S(1)} %copy.12.images_ref, f32[4,8,100]{2,1,0:T(8,128)S(1)} %copy-done), custom_call_target="tpu_custom_call" | custom-call | tf_op jit(solution)/shard_map/targets/pallas_call | solution.py:392
  23.5 9.0 %all-to-all-done = f32[64,1,384]{2,1,0:T(1,128)S(1)} async-done(((f32[64,1,384]{2,1,0:T(1,128)}), f32[64,1,384]{2,1,0:T(1,128)S(1)}, u32[]{:S(2)}, u32[]{:S(2)}) %all-to-all-start) | async-done | bytes 98336 | tf_op jit(solution)/shard_map/all_to_all | solution.py:501
  32.5 0.8 pick.1
  33.3 3.9 %all-to-all-start.1 = ((f32[32,3,4,128]{3,2,1,0:T(4,128)}), f32[32,3,4,128]{3,2,1,0:T(4,128)S(1)}, u32[]{:S(2)}, u32[]{:S(2)}) async-start(f32[32,3,4,128]{3,2,1,0:T(4,128)} %bitcast.5), calls=%async_computation.1 | async-start | bytes 393216 | tf_op jit(solution)/shard_map/all_to_all | solution.py:507
  37.2 2.3 %collective-permute-start = (f32[6,8,8,128]{3,2,1,0:T(8,128)S(1)}, f32[6,8,8,128]{3,2,1,0:T(8,128)S(1)}, u32[]{:S(2)}, u32[]{:S(2)}) collective-permute-start(f32[6,8,8,128]{3,2,1,0:T(8,128)S(1)} %get-tuple-element.13.own_ref), channel_id=1, source_target_pairs={{0,8},{8,0},{16,24},{24,16},{32,40},{40,32},{48,56},{56,48},{64,72... | collective-permute-start | bytes 589832 | tf_op jit(solution)/shard_map/ppermute | solution.py:504
  39.5 0.7 fusion
  40.1 0.1 copy.13.label_ref
  40.2 0.3 collective-permute-done.other_ref
  40.5 8.2 %all-to-all-done.1 = f32[32,3,4,128]{3,2,1,0:T(4,128)S(1)} async-done(((f32[32,3,4,128]{3,2,1,0:T(4,128)}), f32[32,3,4,128]{3,2,1,0:T(4,128)S(1)}, u32[]{:S(2)}, u32[]{:S(2)}) %all-to-all-start.1) | async-done | bytes 196640 | tf_op jit(solution)/shard_map/all_to_all | solution.py:507
  48.8 10.4 %pairs.1 = (f32[16,16,128]{2,1,0:T(8,128)S(1)}, f32[4,4,2,4,8,8,128]{6,5,4,3,2,1,0:T(8,128)S(1)}, f32[2,8,8,8,128]{4,3,2,1,0:T(8,128)S(1)}) custom-call(s32[1]{0:T(128)} %bitcast.core_ref, f32[6,8,8,128]{3,2,1,0:T(8,128)S(1)} %get-tuple-element.13.own_ref, f32[6,8,8,128]{3,2,1,0:T(8,128)S(1)} %collective-permute-done.other_ref, f32[384,128]{1,0:T(8,128)S(1)} %bitcast.25, ...), custom_call_target="tpu_custom_call" | custom-call | tf_op jit(solution)/shard_map/pairs/pallas_call | solution.py:445
  59.2 12.7 %all_to_all.25.parts_ref = f32[16,16,128]{2,1,0:T(8,128)S(1)} all-to-all(f32[16,16,128]{2,1,0:T(8,128)S(1)} %get-tuple-element.17), channel_id=1, replica_groups={{0,1,2,3,4,5,6,7,8,9,10,11,12,13,14,15},{16,17,18,19,20,21,22,23,24,25,..., dimensions={0} | all-to-all | bytes 262144 | tf_op jit(solution)/shard_map/all_to_all | solution.py:514
  71.8 1.7 %weigh.1 = f32[384,128]{1,0:T(8,128)S(1)} custom-call(s32[1]{0:T(128)} %bitcast.core_ref, f32[16,16,128]{2,1,0:T(8,128)S(1)} %all_to_all.25.parts_ref, f32[4,4,2,4,8,8,128]{6,5,4,3,2,1,0:T(8,128)S(1)} %get-tuple-element.18.unit_ref, f32[6,8,8,128]{3,2,1,0:T(8,128)S(1)} %get-tuple-element.13.own_ref, f32[6,8,8,128]{3,2,1,0:T(8,128)S(1)} %collective-permute-done.other_ref, ...), custom_call_target="tpu_custom_call" | custom-call | tf_op jit(solution)/shard_map/weigh/pallas_call | solution.py:471
  73.5 15.3 %all_to_all.26 = f32[32,3,4,128]{3,2,1,0:T(4,128)S(1)} all-to-all(f32[32,3,4,128]{3,2,1,0:T(4,128)S(1)} %bitcast.22), channel_id=1, replica_groups={{0,16,32,48,64,80,96,112,128,144,160,176,192,208,224,240,256,272,288,30..., dimensions={0} | all-to-all | bytes 393216 | tf_op jit(solution)/shard_map/all_to_all | solution.py:518
  88.8 0.1 fold.1
  88.9 16.8 %all_to_all.27 = f32[32,3,4,128]{3,2,1,0:T(4,128)S(1)} all-to-all(f32[32,3,4,128]{3,2,1,0:T(4,128)S(1)} %bitcast.24), channel_id=1, replica_groups={{0,16,32,48,64,80,96,112,128,144,160,176,192,208,224,240,256,272,288,30..., dimensions={0} | all-to-all | bytes 393216 | tf_op jit(solution)/shard_map/all_to_all | solution.py:522
  105.7 4.4 %collective-permute-start.1 = (f32[32,3,4,128]{3,2,1,0:T(4,128)S(1)}, f32[32,3,4,128]{3,2,1,0:T(4,128)S(1)}, u32[]{:S(2)}, u32[]{:S(2)}) collective-permute-start(f32[32,3,4,128]{3,2,1,0:T(4,128)S(1)} %all_to_all.27), channel_id=1, source_target_pairs={{0,8},{8,0},{16,24},{24,16},{32,40},{40,32},{48,56},{56,48},{64,72... | collective-permute-start | bytes 589832 | tf_op jit(solution)/shard_map/ppermute | solution.py:525
  110.2 0.6 dynamic-slice_reduce_fusion
  110.8 0.4 collective-permute-done.1
  111.2 0.1 broadcast_select_fusion.1
  111.3 0.1 copy.14
  111.3 0.1 copy.15
  111.5 0.8 reshape.40
  (1 shorter events, 0.0 us)
Async XLA Ops:
  2.2 30.3 %all-to-all-start = ((f32[64,1,384]{2,1,0:T(1,128)}), f32[64,1,384]{2,1,0:T(1,128)S(1)}, u32[]{:S(2)}, u32[]{:S(2)}) async-start(f32[64,1,384]{2,1,0:T(1,128)} %bitcast.29), calls=%async_computation | async-start | bytes 196608 | tf_op jit(solution)/shard_map/all_to_all | solution.py:501
  20.8 0.7 copy-start
  21.5 0.7 copy-start.1
  33.3 15.5 %all-to-all-start.1 = ((f32[32,3,4,128]{3,2,1,0:T(4,128)}), f32[32,3,4,128]{3,2,1,0:T(4,128)S(1)}, u32[]{:S(2)}, u32[]{:S(2)}) async-start(f32[32,3,4,128]{3,2,1,0:T(4,128)} %bitcast.5), calls=%async_computation.1 | async-start | bytes 393216 | tf_op jit(solution)/shard_map/all_to_all | solution.py:507
  37.2 3.4 %collective-permute-start = (f32[6,8,8,128]{3,2,1,0:T(8,128)S(1)}, f32[6,8,8,128]{3,2,1,0:T(8,128)S(1)}, u32[]{:S(2)}, u32[]{:S(2)}) collective-permute-start(f32[6,8,8,128]{3,2,1,0:T(8,128)S(1)} %get-tuple-element.13.own_ref), channel_id=1, source_target_pairs={{0,8},{8,0},{16,24},{24,16},{32,40},{40,32},{48,56},{56,48},{64,72... | collective-permute-start | bytes 589832 | tf_op jit(solution)/shard_map/ppermute | solution.py:504
  105.7 5.5 %collective-permute-start.1 = (f32[32,3,4,128]{3,2,1,0:T(4,128)S(1)}, f32[32,3,4,128]{3,2,1,0:T(4,128)S(1)}, u32[]{:S(2)}, u32[]{:S(2)}) collective-permute-start(f32[32,3,4,128]{3,2,1,0:T(4,128)S(1)} %all_to_all.27), channel_id=1, source_target_pairs={{0,8},{8,0},{16,24},{24,16},{32,40},{40,32},{48,56},{56,48},{64,72... | collective-permute-start | bytes 589832 | tf_op jit(solution)/shard_map/ppermute | solution.py:525
